TPU v7x, 32 devices: a whole 2x2x4 slice. The times are simulated.
32 devices in a mesh: row: 4 (over y, x), col: 4 (over z), layer: 2 (over core).
Axes of the slice: x: 2, y: 2, z: 4, core: 2. Of those that a mesh axis runs over, the one named last changes fastest.
Arguments:
- earlier_warming_amount: float32 [8, 512, 512], P('layer', 'row', 'col'), may hold values from -2 to 2
- conductive_capability: float32 [8, 512, 512], P('layer', 'row', 'col'), may hold values from 0.5 to 2
- thermal_mass_timewise: float32 [8, 512, 512], P('layer', 'row', 'col'), may hold values from 0.5 to 2
- toggling_wattage_map: bfloat16 [32, 64, 4096], P(('row', 'col', 'layer')), may hold values from 0.049804688 to 1
- baseline_loss_wattage: bfloat16 [32, 64, 4096], P(('row', 'col', 'layer')), may hold values from 0.049804688 to 1
- receiving_panel: int32 [32, 64, 1], P(('row', 'col', 'layer')), may hold values from 0 to 15; in each aligned block of 64 rows (0 to 63, 64 to 127, ..., all dimensions but the last counted through in order) at most 4 rows name the same one
- subsquare_placement: int32 [32, 64], P(('row', 'col', 'layer')), may hold values from 0 to 3
- holder_chip_module: int32 [32, 64], P(('row', 'col', 'layer')), may hold values from 0 to 15, never falling along the last dimension, each value on 1 to 8 neighbouring positions
- module_tier_order: int32 [32, 16], P(('row', 'col', 'layer')), may hold values from 0 to 3
- warming_sensitivity: float32 [32, 16], P(('row', 'col', 'layer')), may hold values from 0.5 to 2
Outputs:
- new_temperature: float32 [8, 512, 512], P('layer', 'row', 'col')
- supplied_wattage_density: float32 [8, 512, 512], P('layer', 'row', 'col')
Inputs may be any that keep to these rules, and one draw needn't show every extreme that they name: `receiving_panel`: the tile is numbered row tile times the number of column tiles plus column tile, inside the owning device's layer group; among the slots of one device at most 4 name the same tile, and exactly 4 do on some device in every draw. `subsquare_placement`: row-major over the tile's patch rows and patch columns. `holder_chip_module`: never falls along a device's slots; every block of a device has 1 to 8 slots.
All inputs are finite; a program needn't handle non-finite values.
Results may differ from a plain program's by a relative error of at most 0.0012.
Values may be sent and summed in bfloat16 or wider, within the bound.
A program may use at most 64 MiB of HBM per device.

v0:
```python
import functools
import jax
import jax.numpy as jnp
from jax import lax
from jax.experimental import pallas as pl
from jax.experimental.pallas import tpu as pltpu
from jax.sharding import PartitionSpec as P

SUB = 64
SWEEPS = 3
CAP = 4
EIG_LOW = 0.1
EIG_HIGH = 2.0
LANES = 128
PACK = 16
VMEM_BYTES = 16 << 20

MESH = pl.DeviceIdType.MESH
F32 = jnp.float32
BF16 = jnp.bfloat16


def iota(shape, dim):
    return lax.broadcasted_iota(jnp.int32, shape, dim)


def hi_dot(a, b, dims):
    return lax.dot_general(
        a, b, (dims, ((), ())), precision=lax.Precision.HIGHEST, preferred_element_type=F32
    )


def div(x, n):
    if n & (n - 1):
        return x // n
    return lax.shift_right_logical(x, jnp.int32(n.bit_length() - 1))


def mod(x, n):
    if n & (n - 1):
        return lax.rem(x, n)
    return x & (n - 1)


def two_parts(x, axis):
    head = x.astype(BF16)
    return jnp.concatenate([head, (x - head.astype(F32)).astype(BF16)], axis=axis)


def kernel(
    sizes,
    temp_hbm,
    cond_hbm,
    mass_hbm,
    dyn_hbm,
    leak_hbm,
    panel_hbm,
    place_hbm,
    block_hbm,
    tier_hbm,
    sens_hbm,
    out_ref,
    power_ref,
    panel_ref,
    place_ref,
    block_ref,
    tier_ref,
    sens_ref,
    temp,
    cond,
    mass,
    dyn,
    leak,
    note_send,
    note_recv,
    load_send,
    load_recv,
    dirs,
    faces,
    diag,
    inv,
    resid,
    edge_send,
    edge_recv,
    plane_recv,
    in_sem,
    note_ssem,
    note_rsem,
    load_ssem,
    load_rsem,
    halo_ssem,
    halo_rsem,
):
    n_row, n_col, n_layer = sizes
    tiles = n_row * n_col
    tiers, rows, cols = temp.shape
    slots, cells = dyn.shape
    folds = PACK // CAP
    wide = cells // folds
    note_rows = note_send.shape[0] // tiles
    in_plane = (rows // SUB) * (cols // SUB)
    patches = tiers * in_plane
    bands = tiers * (rows // SUB)
    chunks = tiles * PACK // LANES

    my_row = lax.axis_index("row")
    my_col = lax.axis_index("col")
    my_layer = lax.axis_index("layer")
    me = my_row * n_col + my_col

    loads = [
        pltpu.make_async_copy(src, dst, in_sem.at[i])
        for i, (src, dst) in enumerate(
            (
                (panel_hbm, panel_ref),
                (place_hbm, place_ref),
                (block_hbm, block_ref),
                (tier_hbm, tier_ref),
                (sens_hbm, sens_ref),
                (temp_hbm, temp),
                (cond_hbm, cond),
                (dyn_hbm.at[0], dyn),
                (leak_hbm.at[0], leak),
                (mass_hbm, mass),
            )
        )
    ]
    for load in loads:
        load.start()

    def peer(step):
        other = lax.rem(me + step, tiles)
        return other, {"row": other // n_col, "col": lax.rem(other, n_col)}

    sides = (
        (my_layer > 0, {"layer": my_layer - 1}, 0),
        (my_layer < n_layer - 1, {"layer": my_layer + 1}, 1),
        (my_row > 0, {"row": my_row - 1}, 2),
        (my_row < n_row - 1, {"row": my_row + 1}, 3),
        (my_col > 0, {"col": my_col - 1}, 4),
        (my_col < n_col - 1, {"col": my_col + 1}, 5),
    )

    barrier = pltpu.get_barrier_semaphore()

    @pl.loop(1, tiles)
    def _(step):
        _, where = peer(step)
        pl.semaphore_signal(barrier, inc=1, device_id=where, device_id_type=MESH)

    for exists, where, side in sides[:2]:

        @pl.when(exists)
        def _(where=where):
            pl.semaphore_signal(barrier, inc=1, device_id=where, device_id_type=MESH)

    for turn in range(4):
        for exists, _, side in sides:

            @pl.when(jnp.logical_not(exists))
            def _(turn=turn, side=side):
                if side < 2:
                    plane_recv[turn, side] = jnp.zeros((rows, cols), F32)
                else:
                    edge_recv[turn, side - 2] = jnp.zeros(edge_recv.shape[2:], F32)

    lane_s = iota((slots, slots), 1)
    sub_s = iota((slots, slots), 0)
    eye = lane_s == sub_s

    def to_col(row):
        return jnp.sum(jnp.where(eye, jnp.broadcast_to(row, (slots, slots)), 0.0), axis=1, keepdims=True)

    def to_row(col):
        return jnp.sum(jnp.where(eye, jnp.broadcast_to(col, (slots, slots)), 0.0), axis=0, keepdims=True)

    for load in loads[:5]:
        load.wait()
    tgt_row = panel_ref[...].astype(F32)
    tgt_col = to_col(tgt_row)
    blk_row = block_ref[...].astype(F32)
    blk_col = to_col(blk_row)
    sub_col = to_col(place_ref[...].astype(F32))
    same_tile = tgt_col == tgt_row
    rank_col = jnp.sum(jnp.where(same_tile & (lane_s < sub_s), 1.0, 0.0), axis=1, keepdims=True)
    rank_row = jnp.sum(jnp.where(same_tile & (sub_s < lane_s), 1.0, 0.0), axis=0, keepdims=True)
    blocks = tier_ref.shape[1]
    of_block = blk_col == iota((slots, blocks), 1).astype(F32)
    tier_col = jnp.sum(jnp.where(of_block, tier_ref[...].astype(F32), 0.0), axis=1, keepdims=True)
    sens_col = jnp.sum(jnp.where(of_block, sens_ref[...], 0.0), axis=1, keepdims=True)
    pos_col = tier_col * in_plane + sub_col
    same_block = jnp.where(blk_col == blk_row, 1.0, 0.0)
    block_size = jnp.sum(same_block, axis=1, keepdims=True)

    offset = lax.rem(me * PACK, LANES)
    my_chunk = (me * PACK) // LANES
    rel = iota((slots, LANES), 1) - offset
    fits = (rel >= 0) & (rel < PACK) & ((rel & (CAP - 1)).astype(F32) == rank_col)
    place_lanes = jnp.where(fits, pos_col + 1.0, 0.0)
    note_i = iota((tiles * note_rows, slots), 0)
    to_tile = jnp.where(
        (div(note_i, note_rows).astype(F32) == tgt_row) & (mod(note_i, note_rows) == 1 + my_chunk),
        1.0,
        0.0,
    )
    places = jnp.dot(to_tile.astype(BF16), place_lanes.astype(BF16), preferred_element_type=F32)

    loads[5].wait()
    band_sums = jnp.concatenate(
        [
            jnp.sum(temp[t, b * SUB : (b + 1) * SUB, :], axis=0, keepdims=True)
            for t in range(tiers)
            for b in range(rows // SUB)
        ],
        axis=0,
    )
    lane_b = iota((bands, LANES), 1)
    sub_b = iota((bands, LANES), 0)
    means = jnp.zeros((1, LANES), F32)
    per_band = cols // SUB
    for part in range(per_band):
        total = jnp.sum(jnp.where(div(lane_b, SUB) == part, band_sums, 0.0), axis=1, keepdims=True)
        means = means + jnp.sum(
            jnp.where(lane_b == sub_b * per_band + part, total, 0.0), axis=0, keepdims=True
        )
    means = means * (1.0 / (SUB * SUB))
    note_j = iota((tiles * note_rows, LANES), 0)
    note_send[...] = places + jnp.where(mod(note_j, note_rows) == 0, means, 0.0)

    sub8 = iota((2 * tiers, 2 * cols), 0)
    lane8 = mod(iota((2 * tiers, 2 * cols), 1), cols)
    picks = [
        jnp.where(
            ((sub8 == t) & (lane8 == 0)) | ((sub8 == tiers + t) & (lane8 == cols - 1)), 1.0, 0.0
        ).astype(BF16)
        for t in range(tiers)
    ]

    def halo_copy(turn, field, where, side, lands):
        if side < 2:
            src = field.at[0 if side == 0 else tiers - 1]
            dst = plane_recv.at[turn, lands]
        else:
            src = edge_send.at[turn, (side - 2) // 2]
            dst = edge_recv.at[turn, lands - 2]
        return pltpu.make_async_remote_copy(
            src_ref=src,
            dst_ref=dst,
            send_sem=halo_ssem.at[turn, side],
            recv_sem=halo_rsem.at[turn, lands],
            device_id=where,
            device_id_type=MESH,
        )

    def pack_rows(turn, field):
        for end in range(2):
            at = end * (rows - 1)
            for t in range(tiers):
                edge_send[turn, 0, end * tiers + t : end * tiers + t + 1, :] = field[t, at : at + 1, :]

    def pack_columns(turn, field):
        columns = jnp.zeros((2 * tiers, rows), F32)
        for t in range(tiers):
            columns = columns + lax.dot_general(
                picks[t], two_parts(field[t], 1), (((1,), (1,)), ((), ())), preferred_element_type=F32
            )
        edge_send[turn, 1] = columns

    def each_side(act, which=sides):
        for exists, where, side in which:
            pl.when(exists)(functools.partial(act, where, side))

    def start_halo(turn, field):
        def start(where, side):
            halo_copy(turn, field, where, side, side ^ 1).start()

        pack_rows(turn, field)
        each_side(start, sides[2:4])
        each_side(start, sides[:2])
        pack_columns(turn, field)
        each_side(start, sides[4:])

    def wait_halo(turn, field):
        each_side(lambda where, side: halo_copy(turn, field, where, side, side).wait_recv())

    def end_halo(turn, field):
        each_side(lambda where, side: halo_copy(turn, field, where, side, side ^ 1).wait_send())

    row_i = iota((rows, cols), 0)
    col_i = iota((rows, cols), 1)
    sub16 = mod(iota((8 * tiers, tiers * cols), 0), 4 * tiers)
    lane16 = iota((8 * tiers, tiers * cols), 1)
    put = jnp.where(
        ((mod(lane16, cols) == 0) & (sub16 == tiers + div(lane16, cols)))
        | ((mod(lane16, cols) == cols - 1) & (sub16 == 2 * tiers + div(lane16, cols))),
        1.0,
        0.0,
    ).astype(BF16)

    def inside(field, t):
        v = field[t]
        none = jnp.zeros_like(v)
        low = none if t == 0 else field[t - 1]
        high = none if t == tiers - 1 else field[t + 1]
        north = jnp.where(row_i == 0, 0.0, pltpu.roll(v, 1, 0))
        south = jnp.where(row_i == rows - 1, 0.0, pltpu.roll(v, rows - 1, 0))
        west = jnp.where(col_i == 0, 0.0, pltpu.roll(v, 1, 1))
        east = jnp.where(col_i == cols - 1, 0.0, pltpu.roll(v, cols - 1, 1))
        return v, (low, high, north, south, west, east)

    def rims(turn):
        ends = jnp.concatenate([edge_recv[turn, 2], edge_recv[turn, 3]], axis=0)
        return lax.dot_general(
            two_parts(ends, 0), put, (((0,), (0,)), ((), ())), preferred_element_type=F32
        )

    def apply_inside(field, t):
        v, around = inside(field, t)
        value = diag[t] * v
        for k in range(6):
            if not (k == 0 and t == 0 or k == 1 and t == tiers - 1):
                value = value - faces[k, t] * around[k]
        return value

    def add_beyond(turn):
        rim = rims(turn)
        resid[0] = resid[0] + faces[0, 0] * plane_recv[turn, 0]
        resid[tiers - 1] = resid[tiers - 1] + faces[1, tiers - 1] * plane_recv[turn, 1]
        for t in range(tiers):
            first, last = slice(0, 1), slice(rows - 1, rows)
            resid[t, first, :] = (
                resid[t, first, :] + faces[2, t, first, :] * edge_recv[turn, 0, tiers + t : tiers + t + 1, :]
            )
            resid[t, last, :] = (
                resid[t, last, :] + faces[3, t, last, :] * edge_recv[turn, 1, t : t + 1, :]
            )
            face = jnp.where(col_i == 0, faces[4, t], faces[5, t])
            resid[t] = resid[t] + face * rim[:, t * cols : (t + 1) * cols]

    beyond = (my_layer > 0).astype(jnp.int32) + (my_layer < n_layer - 1).astype(jnp.int32)
    pl.semaphore_wait(barrier, tiles - 1 + beyond)

    def note_copy(step):
        other, where = peer(step)
        return pltpu.make_async_remote_copy(
            src_ref=note_send.at[pl.ds(other * note_rows, note_rows), :],
            dst_ref=note_recv.at[pl.ds(me * note_rows, note_rows), :],
            send_sem=note_ssem.at[step],
            recv_sem=note_rsem.at[step],
            device_id=where,
            device_id_type=MESH,
        )

    def load_copy(other, lands):
        return pltpu.make_async_remote_copy(
            src_ref=load_send.at[pl.ds(other * PACK, PACK), :],
            dst_ref=load_recv.at[pl.ds(me * PACK, PACK), :],
            send_sem=load_ssem.at[other],
            recv_sem=load_rsem.at[lands],
            device_id={"row": div(other, n_col), "col": mod(other, n_col)},
            device_id_type=MESH,
        )

    @pl.loop(1, tiles)
    def _(step):
        note_copy(step).start()

    own_note = pl.ds(pl.multiple_of(me * note_rows, note_rows), note_rows)
    own_copy = pltpu.make_async_copy(note_send.at[own_note, :], note_recv.at[own_note, :], note_rsem.at[0])
    own_copy.start()

    loads[6].wait()
    start_halo(0, temp)
    start_halo(1, cond)
    loads[7].wait()
    loads[8].wait()
    note_k = iota((slots, tiles * note_rows), 1)
    from_tile = jnp.where(
        (div(note_k, note_rows).astype(F32) == tgt_col) & (mod(note_k, note_rows) == 0), 1.0, 0.0
    )
    at_place = iota((slots, LANES), 1).astype(F32) == pos_col
    send_i = iota((tiles * PACK, folds * slots), 0)
    send_j = iota((tiles * PACK, folds * slots), 1)
    slot_place = jnp.concatenate([tgt_row * CAP + rank_row] * folds, axis=1)
    goes = (div(send_i, PACK) * CAP + mod(send_i, CAP)).astype(F32) == slot_place
    pick = jnp.where(goes & (div(mod(send_i, PACK), CAP) == div(send_j, slots)), 1.0, 0.0).astype(BF16)
    own_copy.wait()

    @pl.loop(1, tiles)
    def _(step):
        note_copy(step).wait_recv()

    tile_means = hi_dot(from_tile, note_recv[...], ((1,), (0,)))
    slot_mean = jnp.sum(jnp.where(at_place, tile_means, 0.0), axis=1, keepdims=True)
    block_rise = jnp.sum(same_block * to_row(slot_mean), axis=1, keepdims=True) / block_size
    factor = jnp.exp(sens_col * block_rise)
    half = wide // 2
    for piece in range(2):
        slot_power = jnp.concatenate(
            [
                (
                    dyn[:, fold * wide + piece * half : fold * wide + (piece + 1) * half].astype(F32)
                    + factor
                    * leak[:, fold * wide + piece * half : fold * wide + (piece + 1) * half].astype(F32)
                ).astype(BF16)
                for fold in range(folds)
            ],
            axis=0,
        )
        load_send[:, piece * half : (piece + 1) * half] = jnp.dot(
            pick, slot_power, preferred_element_type=F32
        ).astype(BF16)

    @pl.loop(0, tiles)
    def _(step):
        nth = div(step, n_row)
        far = jnp.where(my_col < n_col // 2, n_col - 1 - nth, nth)
        other = lax.rem(my_row + lax.rem(step, n_row), n_row) * n_col + far

        @pl.when(other != me)
        def _():
            load_copy(other, me).start()

    own_load = pl.ds(pl.multiple_of(me * PACK, PACK), PACK)
    own_move = pltpu.make_async_copy(load_send.at[own_load, :], load_recv.at[own_load, :], load_rsem.at[me])
    own_move.start()

    loads[9].wait()
    wait_halo(0, temp)
    wait_halo(1, cond)
    rim = rims(1)
    for t in range(tiers):
        c, (low, high, north, south, west, east) = inside(cond, t)
        here = rim[:, t * cols : (t + 1) * cols]
        low = plane_recv[1, 0] if t == 0 else low
        high = plane_recv[1, 1] if t == tiers - 1 else high
        north = jnp.where(row_i == 0, edge_recv[1, 0, tiers + t : tiers + t + 1, :], north)
        south = jnp.where(row_i == rows - 1, edge_recv[1, 1, t : t + 1, :], south)
        west = jnp.where(col_i == 0, here, west)
        east = jnp.where(col_i == cols - 1, here, east)
        total = mass[t]
        for k, beside in enumerate((low, high, north, south, west, east)):
            face = 0.5 * (c + beside)
            faces[k, t] = face
            total = total + face
        diag[t] = total
        inv[t] = 1.0 / total
    for t in range(tiers):
        resid[t] = mass[t] * temp[t] - apply_inside(temp, t)
    add_beyond(0)

    middle = (EIG_LOW + EIG_HIGH) / 2.0
    spread = (EIG_HIGH - EIG_LOW) / 2.0
    ratio = middle / spread
    weight = 1.0 / ratio

    sel_i = iota((folds * patches, LANES), 0)
    sel_j = iota((folds * patches, LANES), 1)
    sel_in = mod(sel_i, patches)
    sel_patch = mod(sel_in, bands) * per_band + div(sel_in, bands)
    fold_hit = div(sel_i, patches) == div(mod(sel_j, PACK), CAP)
    notes = note_recv[...]
    pickers = []
    for chunk in range(chunks):
        code = jnp.sum(jnp.where(mod(note_j, note_rows) == 1 + chunk, notes, 0.0), axis=0, keepdims=True)
        pickers.append(
            jnp.where(fold_hit & (code == (sel_patch + 1).astype(F32)), 1.0, 0.0).astype(BF16)
        )

    picker = jnp.concatenate(pickers, axis=1)
    own_move.wait()

    @pl.loop(1, tiles)
    def _(step):
        other, _ = peer(step)
        load_copy(other, other).wait_recv()

    footprint = jnp.dot(picker, load_recv[...], preferred_element_type=F32)
    left = iota((bands, LANES), 1) < SUB
    for fold in range(folds):
        for k in range(wide // LANES):
            lanes = slice(k * LANES, (k + 1) * LANES)
            a = footprint[fold * patches : fold * patches + bands, lanes]
            b = footprint[fold * patches + bands : fold * patches + 2 * bands, lanes]
            at = 2 * (fold * (wide // LANES) + k)
            power_ref[pl.ds(at, bands, stride=SUB), :] = jnp.where(left, a, pltpu.roll(b, SUB, 1))
            power_ref[pl.ds(at + 1, bands, stride=SUB), :] = jnp.where(left, pltpu.roll(a, SUB, 1), b)

    for t in range(tiers):
        r = resid[t] + power_ref[t * rows : (t + 1) * rows, :]
        resid[t] = r
        dirs[0, t] = r * inv[t] * (1.0 / middle)
    for sweep in range(1, SWEEPS):
        field = dirs.at[sweep - 1]
        turn = 1 + sweep
        start_halo(turn, field)
        weight_new = 1.0 / (2.0 * ratio - weight)
        for t in range(tiers):
            base = temp[t] if sweep == 1 else out_ref[t]
            out_ref[t] = base + field[t]
            resid[t] = resid[t] - apply_inside(field, t)
        wait_halo(turn, field)
        add_beyond(turn)
        for t in range(tiers):
            d = weight_new * weight * field[t] + (2.0 * weight_new / spread) * (resid[t] * inv[t])
            if sweep < SWEEPS - 1:
                dirs[sweep, t] = d
            else:
                out_ref[t] = out_ref[t] + d
        weight = weight_new
    end_halo(0, temp)
    end_halo(1, cond)
    for sweep in range(1, SWEEPS):
        end_halo(1 + sweep, dirs.at[sweep - 1])

    @pl.loop(1, tiles)
    def _(step):
        note_copy(step).wait_send()
        other, _ = peer(step)
        load_copy(other, me).wait_send()


def hand_over(new, power, new_out, power_out, sem):
    moves = (pltpu.make_async_copy(power, power_out, sem.at[0]), pltpu.make_async_copy(new, new_out, sem.at[1]))
    for move in moves:
        move.start()
    for move in moves:
        move.wait()


def shards(sizes, temp, cond, mass, dyn, leak, panel, place, block, tier, sens):
    tiers, rows, cols = temp.shape
    slots, cells = dyn.shape[1:]
    tiles = sizes[0] * sizes[1]
    folds = PACK // CAP
    note_rows = -(-(1 + tiles * PACK // LANES) // 8) * 8
    any_spec = pl.BlockSpec(memory_space=pl.ANY)
    vmem_spec = pl.BlockSpec(memory_space=pltpu.VMEM)
    grid = (tiers, rows, cols)
    dma = pltpu.SemaphoreType.DMA
    new, power = pl.pallas_call(
        functools.partial(kernel, sizes),
        out_shape=(
            pltpu.VMEM(grid, F32),
            pltpu.VMEM((tiers * rows, cols), F32),
        ),
        in_specs=[any_spec] * 10,
        out_specs=(vmem_spec, vmem_spec),
        scratch_shapes=[
            pltpu.VMEM((1, slots), jnp.int32),
            pltpu.VMEM((1, slots), jnp.int32),
            pltpu.VMEM((1, slots), jnp.int32),
            pltpu.VMEM(tier.shape, jnp.int32),
            pltpu.VMEM(sens.shape, F32),
            pltpu.VMEM(grid, F32),
            pltpu.VMEM(grid, F32),
            pltpu.VMEM(grid, F32),
            pltpu.VMEM((slots, cells), BF16),
            pltpu.VMEM((slots, cells), BF16),
            pltpu.VMEM((tiles * note_rows, LANES), F32),
            pltpu.VMEM((tiles * note_rows, LANES), F32),
            pltpu.VMEM((tiles * PACK, cells // folds), BF16),
            pltpu.VMEM((tiles * PACK, cells // folds), BF16),
            pltpu.VMEM((SWEEPS - 1,) + grid, F32),
            pltpu.VMEM((6,) + grid, F32),
            pltpu.VMEM(grid, F32),
            pltpu.VMEM(grid, F32),
            pltpu.VMEM(grid, F32),
            pltpu.VMEM((SWEEPS + 1, 2, 2 * tiers, cols), F32),
            pltpu.VMEM((SWEEPS + 1, 4, 2 * tiers, cols), F32),
            pltpu.VMEM((SWEEPS + 1, 2, rows, cols), F32),
            dma((10,)),
            dma((tiles,)),
            dma((tiles,)),
            dma((tiles,)),
            dma((tiles,)),
            dma((SWEEPS + 1, 6)),
            dma((SWEEPS + 1, 6)),
        ],
        compiler_params=pltpu.CompilerParams(
            collective_id=0, has_side_effects=True, vmem_limit_bytes=VMEM_BYTES
        ),
    )(
        *(
            pltpu.with_memory_space_constraint(given, pltpu.HBM)
            for given in (temp, cond, mass, dyn, leak, panel.reshape(1, slots), place, block, tier, sens)
        )
    )
    return pl.pallas_call(
        hand_over,
        out_shape=(jax.ShapeDtypeStruct(grid, F32),) * 2,
        in_specs=[vmem_spec] * 2,
        out_specs=(any_spec, any_spec),
        scratch_shapes=[dma((2,))],
        compiler_params=pltpu.CompilerParams(vmem_limit_bytes=VMEM_BYTES),
    )(new, power.reshape(grid))


def solution(mesh):
    sizes = (mesh.shape["row"], mesh.shape["col"], mesh.shape["layer"])
    owner = ("row", "col", "layer")
    return jax.shard_map(
        functools.partial(shards, sizes),
        mesh=mesh,
        in_specs=(P("layer", "row", "col"),) * 3
        + (P(owner, None, None),) * 3
        + (P(owner, None),) * 4,
        out_specs=(P("layer", "row", "col"), P("layer", "row", "col")),
        check_vma=False,
    )
```

profile of v0, /device:TPU:0, one launch (start us, length us, event | category | flops | bytes accessed | tf_op | source)
XLA Modules:
  0.0 33.7 jit_solution(4469896661468957672)
XLA Ops:
  0.6 32.3 %shard_map.113 = (f32[4,128,128]{2,1,0:T(8,128)S(1)}, f32[512,128]{1,0:T(8,128)S(1)}) custom-call(f32[4,128,128]{2,1,0:T(8,128)} %temp_hbm.1, f32[4,128,128]{2,1,0:T(8,128)} %cond_hbm.1, f32[4,128,128]{2,1,0:T(8,128)} %mass_hbm.1, bf16[1,64,4096]{2,1,0:T(8,128)(2,1)} %dyn_hbm.1, bf16[1,64,4096]{2,1,0:T(8,128)(2,1)} %leak_hbm.1, s32[1,64]{1,0:T(1,128)} %bitcast.3, ...), custom_call_target="tpu_custom_call" | custom-call | tf_op jit(solution)/shard_map/pallas_call | solution.py:541
  32.9 0.8 %shard_map.114 = (f32[4,128,128]{2,1,0:T(8,128)}, f32[4,128,128]{2,1,0:T(8,128)}) custom-call(f32[4,128,128]{2,1,0:T(8,128)S(1)} %get-tuple-element.4.new, f32[4,128,128]{2,1,0:T(8,128)S(1)} %bitcast.2), custom_call_target="tpu_custom_call" | custom-call | tf_op jit(solution)/shard_map/pallas_call | solution.py:589
where the time goes:
time: 33.9 us; the launch traced here: 33.7 us
  Pallas kernels  33.1 us (98%)
  between operations  0.64 us (2%)
    pallas_call x1, Pallas kernels, shards(): pl.pallas_call(functools.partial(kernel, sizes), out_shape=(pltpu.VMEM(gr...  32.3 us
    pallas_call x1, Pallas kernels, shards(): pl.pallas_call(hand_over, out_shape=(jax.ShapeDtypeStruct(grid, F32),) *...  0.81 us

commit v1 on v0

v1 whole, which is shorter than its diff:
```python
import functools
import jax
import jax.numpy as jnp
from jax import lax
from jax.experimental import pallas as pl
from jax.experimental.pallas import tpu as pltpu
from jax.sharding import PartitionSpec as P

SUB = 64
SWEEPS = 3
CAP = 4
EIG_LOW = 0.1
EIG_HIGH = 2.0
LANES = 128
FOLDS = 16
VMEM_BYTES = 40 << 20

MESH = pl.DeviceIdType.MESH
F32 = jnp.float32
BF16 = jnp.bfloat16


def iota(shape, dim):
    return lax.broadcasted_iota(jnp.int32, shape, dim)


def div(x, n):
    if n & (n - 1):
        return x // n
    return lax.shift_right_logical(x, jnp.int32(n.bit_length() - 1))


def mod(x, n):
    if n & (n - 1):
        return lax.rem(x, n)
    return x & (n - 1)


def three_parts(x, axis):
    head = x.astype(BF16)
    rest = x - head.astype(F32)
    body = rest.astype(BF16)
    return jnp.concatenate([head, body, (rest - body.astype(F32)).astype(BF16)], axis=axis)


def two_parts(x, axis):
    head = x.astype(BF16)
    return jnp.concatenate([head, (x - head.astype(F32)).astype(BF16)], axis=axis)


def kernel(
    sizes,
    temp_hbm,
    cond_hbm,
    mass_hbm,
    dyn_hbm,
    leak_hbm,
    panel_hbm,
    place_hbm,
    block_hbm,
    tier_hbm,
    sens_hbm,
    out_ref,
    power_ref,
    panel_ref,
    place_ref,
    block_ref,
    tier_ref,
    sens_ref,
    temp,
    cond,
    mass,
    dyn,
    leak,
    dyn_pick,
    leak_pick,
    note_send,
    note_recv,
    place_send,
    place_recv,
    fac,
    load_send,
    load_recv,
    dirs,
    faces,
    diag,
    inv,
    resid,
    edge_send,
    edge_recv,
    plane_recv,
    nothing,
    waste,
    in_sem,
    note_ssem,
    note_rsem,
    place_ssem,
    place_rsem,
    load_ssem,
    load_rsem,
    halo_ssem,
    halo_rsem,
):
    n_row, n_col, n_layer = sizes
    tiles = n_row * n_col
    tiers, rows, cols = temp.shape
    slots, cells = dyn.shape
    wide = cells // FOLDS
    halves = wide // LANES
    named = 8 * tiles
    in_plane = (rows // SUB) * (cols // SUB)
    patches = tiers * in_plane
    bands = tiers * (rows // SUB)
    my_row = lax.axis_index("row")
    my_col = lax.axis_index("col")
    my_layer = lax.axis_index("layer")
    me = my_row * n_col + my_col

    loads = [
        pltpu.make_async_copy(src, dst, in_sem.at[i])
        for i, (src, dst) in enumerate(
            (
                (temp_hbm, temp),
                (panel_hbm, panel_ref),
                (place_hbm, place_ref),
                (block_hbm, block_ref),
                (tier_hbm, tier_ref),
                (sens_hbm, sens_ref),
                (dyn_hbm.at[0], dyn),
                (leak_hbm.at[0], leak),
                (cond_hbm, cond),
                (mass_hbm, mass),
            )
        )
    ]
    for load in loads:
        load.start()

    def far_first(step):
        if n_row & (n_row - 1) or n_col & (n_col - 1) or n_col == 1:
            return lax.rem(me + step, tiles)
        near = n_col // 2
        turn = mod(step, tiles // 2)
        over_row = n_row - 1 - div(turn, near)
        over_col = n_col - 1 - mod(turn, near) - near * div(step, tiles // 2)
        return lax.bitwise_xor(my_row, over_row) * n_col + lax.bitwise_xor(my_col, over_col)

    def each_peer(act):
        @pl.loop(0, tiles)
        def _(step):
            other = far_first(step)
            pl.when(other != me)(lambda: act(other))

    def device(other):
        return {"row": div(other, n_col), "col": mod(other, n_col)}

    sides = (
        (my_layer > 0, {"layer": my_layer - 1}, 0),
        (my_layer < n_layer - 1, {"layer": my_layer + 1}, 1),
        (my_row > 0, {"row": my_row - 1}, 2),
        (my_row < n_row - 1, {"row": my_row + 1}, 3),
        (my_col > 0, {"col": my_col - 1}, 4),
        (my_col < n_col - 1, {"col": my_col + 1}, 5),
    )

    nothing[...] = jnp.zeros_like(nothing)
    barrier = pltpu.get_barrier_semaphore()

    each_peer(
        lambda other: pl.semaphore_signal(barrier, inc=1, device_id=device(other), device_id_type=MESH)
    )

    for exists, where, side in sides[:2]:

        @pl.when(exists)
        def _(where=where):
            pl.semaphore_signal(barrier, inc=1, device_id=where, device_id_type=MESH)

    def remote(src, dst, ssem, rsem, other):
        return pltpu.make_async_remote_copy(
            src_ref=src,
            dst_ref=dst,
            send_sem=ssem,
            recv_sem=rsem,
            device_id=device(other),
            device_id_type=MESH,
        )

    def eight(tile):
        return pl.ds(pl.multiple_of(tile * 8, 8), 8)

    def note_copy(other):
        return remote(note_send, note_recv.at[me], note_ssem, note_rsem, other)

    def place_copy(other):
        return remote(place_send.at[eight(other), :], place_recv.at[eight(me), :], place_ssem, place_rsem, other)

    def load_copy(other):
        return remote(load_send.at[other], load_recv.at[me], load_ssem, load_rsem, other)

    def bytes_of(ref, sem):
        return pltpu.make_async_copy(ref, ref, sem)

    def keep(src, dst, sem):
        pltpu.make_async_copy(src, dst, sem).start()

    loads[0].wait()
    band_sums = jnp.concatenate(
        [
            jnp.sum(temp[t, b * SUB : (b + 1) * SUB, :], axis=0, keepdims=True)
            for t in range(tiers)
            for b in range(rows // SUB)
        ],
        axis=0,
    )
    lane_b = iota((bands, LANES), 1)
    sub_b = iota((bands, LANES), 0)
    means = jnp.zeros((1, LANES), F32)
    per_band = cols // SUB
    for part in range(per_band):
        total = jnp.sum(jnp.where(div(lane_b, SUB) == part, band_sums, 0.0), axis=1, keepdims=True)
        means = means + jnp.sum(
            jnp.where(lane_b == sub_b * per_band + part, total, 0.0), axis=0, keepdims=True
        )
    means = means * (1.0 / (SUB * SUB))
    note_send[...] = means
    beyond = (my_layer > 0).astype(jnp.int32) + (my_layer < n_layer - 1).astype(jnp.int32)
    pl.semaphore_wait(barrier, tiles - 1 + beyond)

    each_peer(lambda other: note_copy(other).start())
    keep(note_send, note_recv.at[me], note_rsem)
    lane_s = iota((slots, slots), 1)
    sub_s = iota((slots, slots), 0)
    eye = lane_s == sub_s

    def to_col(row):
        return jnp.sum(jnp.where(eye, jnp.broadcast_to(row, (slots, slots)), 0.0), axis=1, keepdims=True)

    def to_row(col):
        return jnp.sum(jnp.where(eye, jnp.broadcast_to(col, (slots, slots)), 0.0), axis=0, keepdims=True)

    for load in loads[1:6]:
        load.wait()
    tgt_row = panel_ref[...].astype(F32)
    tgt_col = to_col(tgt_row)
    blk_row = block_ref[...].astype(F32)
    blk_col = to_col(blk_row)
    sub_col = to_col(place_ref[...].astype(F32))
    same_tile = tgt_col == tgt_row
    rank_col = jnp.sum(jnp.where(same_tile & (lane_s < sub_s), 1.0, 0.0), axis=1, keepdims=True)
    rank_row = jnp.sum(jnp.where(same_tile & (sub_s < lane_s), 1.0, 0.0), axis=0, keepdims=True)
    blocks = tier_ref.shape[1]
    of_block = blk_col == iota((slots, blocks), 1).astype(F32)
    tier_col = jnp.sum(jnp.where(of_block, tier_ref[...].astype(F32), 0.0), axis=1, keepdims=True)
    sens_col = jnp.sum(jnp.where(of_block, sens_ref[...], 0.0), axis=1, keepdims=True)
    pos_col = tier_col * in_plane + sub_col
    goes = (tgt_row * CAP + rank_row) == iota((tiles * CAP, slots), 0).astype(F32)
    pick = jnp.where(goes, 1.0, 0.0).astype(BF16)
    sub8 = iota((2 * tiers, 2 * cols), 0)
    lane8 = mod(iota((2 * tiers, 2 * cols), 1), cols)
    picks = [
        jnp.where(
            ((sub8 == t) & (lane8 == 0)) | ((sub8 == tiers + t) & (lane8 == cols - 1)), 1.0, 0.0
        ).astype(BF16)
        for t in range(tiers)
    ]

    def halo_ends(turn, field, side, lands):
        if side < 2:
            return field.at[0 if side == 0 else tiers - 1], plane_recv.at[turn, lands], 0
        return edge_send.at[turn, (side - 2) // 2], edge_recv.at[turn, lands - 2], 1

    def halo_start(turn, field, exists, where, side):
        @pl.when(exists)
        def _():
            src, dst, kind = halo_ends(turn, field, side, side ^ 1)
            pltpu.make_async_remote_copy(
                src_ref=src,
                dst_ref=dst,
                send_sem=halo_ssem.at[kind],
                recv_sem=halo_rsem.at[turn, kind],
                device_id=where,
                device_id_type=MESH,
            ).start()

        @pl.when(jnp.logical_not(exists))
        def _():
            _, dst, kind = halo_ends(turn, field, side, side)
            none = nothing.at[...] if kind == 0 else nothing.at[: 2 * tiers, :]
            spare = waste.at[turn, side]
            spare = spare if kind == 0 else spare.at[: 2 * tiers, :]
            keep(none, dst, halo_rsem.at[turn, kind])
            keep(none, spare, halo_ssem.at[kind])

    def pack_rows(turn, field):
        for end in range(2):
            at = end * (rows - 1)
            for t in range(tiers):
                edge_send[turn, 0, end * tiers + t : end * tiers + t + 1, :] = field[t, at : at + 1, :]

    def pack_columns(turn, field):
        columns = jnp.zeros((2 * tiers, rows), F32)
        for t in range(tiers):
            columns = columns + lax.dot_general(
                picks[t], two_parts(field[t], 1), (((1,), (1,)), ((), ())), preferred_element_type=F32
            )
        edge_send[turn, 1] = columns

    def start_halo(turn, field):
        def start(which):
            for exists, where, side in which:
                halo_start(turn, field, exists, where, side)

        pack_rows(turn, field)
        start(sides[2:4])
        start(sides[:2])
        pack_columns(turn, field)
        start(sides[4:])

    def wait_halo(turn):
        bytes_of(plane_recv.at[turn], halo_rsem.at[turn, 0]).wait()
        bytes_of(edge_recv.at[turn], halo_rsem.at[turn, 1]).wait()

    row_i = iota((rows, cols), 0)
    col_i = iota((rows, cols), 1)
    sub16 = mod(iota((8 * tiers, tiers * cols), 0), 4 * tiers)
    lane16 = iota((8 * tiers, tiers * cols), 1)
    put = jnp.where(
        ((mod(lane16, cols) == 0) & (sub16 == tiers + div(lane16, cols)))
        | ((mod(lane16, cols) == cols - 1) & (sub16 == 2 * tiers + div(lane16, cols))),
        1.0,
        0.0,
    ).astype(BF16)

    def inside(field, t):
        v = field[t]
        none = jnp.zeros_like(v)
        low = none if t == 0 else field[t - 1]
        high = none if t == tiers - 1 else field[t + 1]
        north = jnp.where(row_i == 0, 0.0, pltpu.roll(v, 1, 0))
        south = jnp.where(row_i == rows - 1, 0.0, pltpu.roll(v, rows - 1, 0))
        west = jnp.where(col_i == 0, 0.0, pltpu.roll(v, 1, 1))
        east = jnp.where(col_i == cols - 1, 0.0, pltpu.roll(v, cols - 1, 1))
        return v, (low, high, north, south, west, east)

    def rims(turn):
        ends = jnp.concatenate([edge_recv[turn, 2], edge_recv[turn, 3]], axis=0)
        return lax.dot_general(
            two_parts(ends, 0), put, (((0,), (0,)), ((), ())), preferred_element_type=F32
        )

    def apply_inside(field, t):
        v, around = inside(field, t)
        value = diag[t] * v
        for k in range(6):
            if not (k == 0 and t == 0 or k == 1 and t == tiers - 1):
                value = value - faces[k, t] * around[k]
        return value

    def add_beyond(turn):
        rim = rims(turn)
        resid[0] = resid[0] + faces[0, 0] * plane_recv[turn, 0]
        resid[tiers - 1] = resid[tiers - 1] + faces[1, tiers - 1] * plane_recv[turn, 1]
        for t in range(tiers):
            first, last = slice(0, 1), slice(rows - 1, rows)
            resid[t, first, :] = (
                resid[t, first, :] + faces[2, t, first, :] * edge_recv[turn, 0, tiers + t : tiers + t + 1, :]
            )
            resid[t, last, :] = (
                resid[t, last, :] + faces[3, t, last, :] * edge_recv[turn, 1, t : t + 1, :]
            )
            face = jnp.where(col_i == 0, faces[4, t], faces[5, t])
            resid[t] = resid[t] + face * rim[:, t * cols : (t + 1) * cols]

    name_r = iota((named, slots), 0).astype(F32)
    named_row = tgt_row * 8.0 + rank_row
    named_col = tgt_col * 8.0 + rank_col
    by_name = name_r == named_row

    def rename(row):
        return jnp.sum(jnp.where(by_name, row, 0.0), axis=1, keepdims=True)

    pos_r = rename(to_row(pos_col) + 1.0)
    blk_r = rename(blk_row + 1.0)
    sens_r = rename(to_row(sens_col))
    blk_n = jnp.sum(
        jnp.where(named_col == iota((slots, named), 1).astype(F32), blk_col + 1.0, 0.0), axis=0, keepdims=True
    )
    same_block = jnp.where((blk_r == blk_n) & (blk_r > 0.0), 1.0, 0.0)
    block_size = jnp.maximum(jnp.sum(same_block, axis=1, keepdims=True), 1.0)
    same_three = jnp.concatenate([same_block.astype(BF16)] * 3, axis=1)
    at_place = (iota((named, LANES), 1) + 1).astype(F32) == pos_r
    place_send[...] = jnp.broadcast_to(pos_r, place_send.shape)
    each_peer(lambda other: place_copy(other).start())
    keep(place_send.at[eight(me), :], place_recv.at[eight(me), :], place_rsem)

    loads[8].wait()
    start_halo(0, temp)
    start_halo(1, cond)

    loads[6].wait()
    loads[7].wait()
    for src, dst in ((dyn, dyn_pick), (leak, leak_pick)):
        for fold in range(FOLDS):
            taken = jnp.dot(pick, src[:, fold * wide : (fold + 1) * wide], preferred_element_type=F32)
            for half in range(halves):
                dst[half, pl.ds(fold, tiles * CAP, stride=FOLDS), :] = taken[
                    :, half * LANES : (half + 1) * LANES
                ]

    bytes_of(note_recv, note_rsem).wait()
    tile_means = jnp.concatenate([jnp.broadcast_to(note_recv[tile], (8, LANES)) for tile in range(tiles)], axis=0)
    at_slots = three_parts(jnp.where(at_place, tile_means, 0.0), 0)
    block_sum = jnp.sum(
        jnp.dot(same_three, at_slots, preferred_element_type=F32), axis=1, keepdims=True
    )
    fac[...] = jnp.broadcast_to(jnp.exp(sens_r * (block_sum / block_size)), (named, LANES))

    @pl.loop(0, tiles)
    def _(step):
        other = far_first(step)
        for rank in range(CAP):
            by = fac[pl.ds(other * 8 + rank, 8, stride=0), :]
            by = jnp.concatenate([by] * (FOLDS // 8), axis=0)
            at = pl.ds(pl.multiple_of((other * CAP + rank) * FOLDS, FOLDS), FOLDS)
            for half in range(halves):
                load_send[other, rank * FOLDS : (rank + 1) * FOLDS, half * LANES : (half + 1) * LANES] = (
                    dyn_pick[half, at, :] + by * leak_pick[half, at, :]
                ).astype(BF16)

        @pl.when(other != me)
        def _():
            load_copy(other).start()

    keep(load_send.at[me], load_recv.at[me], load_rsem)

    loads[9].wait()
    wait_halo(0)
    wait_halo(1)
    rim = rims(1)
    for t in range(tiers):
        c, (low, high, north, south, west, east) = inside(cond, t)
        here = rim[:, t * cols : (t + 1) * cols]
        low = plane_recv[1, 0] if t == 0 else low
        high = plane_recv[1, 1] if t == tiers - 1 else high
        north = jnp.where(row_i == 0, edge_recv[1, 0, tiers + t : tiers + t + 1, :], north)
        south = jnp.where(row_i == rows - 1, edge_recv[1, 1, t : t + 1, :], south)
        west = jnp.where(col_i == 0, here, west)
        east = jnp.where(col_i == cols - 1, here, east)
        total = mass[t]
        for k, beside in enumerate((low, high, north, south, west, east)):
            face = 0.5 * (c + beside)
            faces[k, t] = face
            total = total + face
        diag[t] = total
        inv[t] = 1.0 / total
    for t in range(tiers):
        resid[t] = mass[t] * temp[t] - apply_inside(temp, t)
    add_beyond(0)

    middle = (EIG_LOW + EIG_HIGH) / 2.0
    spread = (EIG_HIGH - EIG_LOW) / 2.0
    ratio = middle / spread
    weight = 1.0 / ratio

    sources = tiles * CAP * FOLDS
    sel_i = iota((FOLDS * patches, sources), 0)
    sel_j = iota((FOLDS * patches, sources), 1)
    sel_in = mod(sel_i, patches)
    sel_patch = mod(sel_in, bands) * per_band + div(sel_in, bands)
    fold_hit = div(sel_i, patches) == mod(sel_j, FOLDS)
    bytes_of(place_recv, place_rsem).wait()
    place_i = iota((named, sources), 0)
    place_j = div(iota((named, sources), 1), FOLDS)
    place_j = div(place_j, CAP) * 8 + mod(place_j, CAP)
    places = jnp.concatenate([place_recv[...]] * (sources // LANES), axis=1)
    code = jnp.sum(jnp.where(place_i == place_j, places, 0.0), axis=0, keepdims=True)
    picker = jnp.where(fold_hit & (code == (sel_patch + 1).astype(F32)), 1.0, 0.0).astype(BF16)
    bytes_of(load_recv, load_rsem).wait()
    footprint = jnp.dot(picker, load_recv[...].reshape(sources, wide), preferred_element_type=F32)
    left = iota((bands, LANES), 1) < SUB
    for fold in range(FOLDS):
        for k in range(wide // LANES):
            lanes = slice(k * LANES, (k + 1) * LANES)
            a = footprint[fold * patches : fold * patches + bands, lanes]
            b = footprint[fold * patches + bands : fold * patches + 2 * bands, lanes]
            at = 2 * (fold * (wide // LANES) + k)
            power_ref[pl.ds(at, bands, stride=SUB), :] = jnp.where(left, a, pltpu.roll(b, SUB, 1))
            power_ref[pl.ds(at + 1, bands, stride=SUB), :] = jnp.where(left, pltpu.roll(a, SUB, 1), b)

    for t in range(tiers):
        r = resid[t] + power_ref[t * rows : (t + 1) * rows, :]
        resid[t] = r
        dirs[0, t] = r * inv[t] * (1.0 / middle)
    for sweep in range(1, SWEEPS):
        field = dirs.at[sweep - 1]
        turn = 1 + sweep
        start_halo(turn, field)
        weight_new = 1.0 / (2.0 * ratio - weight)
        for t in range(tiers):
            base = temp[t] if sweep == 1 else out_ref[t]
            out_ref[t] = base + field[t]
            resid[t] = resid[t] - apply_inside(field, t)
        wait_halo(turn)
        add_beyond(turn)
        for t in range(tiers):
            d = weight_new * weight * field[t] + (2.0 * weight_new / spread) * (resid[t] * inv[t])
            if sweep < SWEEPS - 1:
                dirs[sweep, t] = d
            else:
                out_ref[t] = out_ref[t] + d
        weight = weight_new
    bytes_of(plane_recv, halo_ssem.at[0]).wait()
    bytes_of(edge_recv, halo_ssem.at[1]).wait()
    bytes_of(note_recv.at[1:], note_ssem).wait()
    bytes_of(place_recv.at[8:, :], place_ssem).wait()
    bytes_of(load_recv.at[1:], load_ssem).wait()


def hand_over(new, power, new_out, power_out, sem):
    moves = (pltpu.make_async_copy(power, power_out, sem.at[0]), pltpu.make_async_copy(new, new_out, sem.at[1]))
    for move in moves:
        move.start()
    for move in moves:
        move.wait()


def shards(sizes, temp, cond, mass, dyn, leak, panel, place, block, tier, sens):
    tiers, rows, cols = temp.shape
    slots, cells = dyn.shape[1:]
    tiles = sizes[0] * sizes[1]
    any_spec = pl.BlockSpec(memory_space=pl.ANY)
    vmem_spec = pl.BlockSpec(memory_space=pltpu.VMEM)
    grid = (tiers, rows, cols)
    dma = pltpu.SemaphoreType.DMA
    new, power = pl.pallas_call(
        functools.partial(kernel, sizes),
        out_shape=(
            pltpu.VMEM(grid, F32),
            pltpu.VMEM((tiers * rows, cols), F32),
        ),
        in_specs=[any_spec] * 10,
        out_specs=(vmem_spec, vmem_spec),
        scratch_shapes=[
            pltpu.VMEM((1, slots), jnp.int32),
            pltpu.VMEM((1, slots), jnp.int32),
            pltpu.VMEM((1, slots), jnp.int32),
            pltpu.VMEM(tier.shape, jnp.int32),
            pltpu.VMEM(sens.shape, F32),
            pltpu.VMEM(grid, F32),
            pltpu.VMEM(grid, F32),
            pltpu.VMEM(grid, F32),
            pltpu.VMEM((slots, cells), BF16),
            pltpu.VMEM((slots, cells), BF16),
            pltpu.VMEM((cells // FOLDS // LANES, tiles * CAP * FOLDS, LANES), F32),
            pltpu.VMEM((cells // FOLDS // LANES, tiles * CAP * FOLDS, LANES), F32),
            pltpu.VMEM((1, LANES), F32),
            pltpu.VMEM((tiles, 1, LANES), F32),
            pltpu.VMEM((8 * tiles, LANES), F32),
            pltpu.VMEM((8 * tiles, LANES), F32),
            pltpu.VMEM((8 * tiles, LANES), F32),
            pltpu.VMEM((tiles, CAP * FOLDS, cells // FOLDS), BF16),
            pltpu.VMEM((tiles, CAP * FOLDS, cells // FOLDS), BF16),
            pltpu.VMEM((SWEEPS - 1,) + grid, F32),
            pltpu.VMEM((6,) + grid, F32),
            pltpu.VMEM(grid, F32),
            pltpu.VMEM(grid, F32),
            pltpu.VMEM(grid, F32),
            pltpu.VMEM((SWEEPS + 1, 2, 2 * tiers, cols), F32),
            pltpu.VMEM((SWEEPS + 1, 4, 2 * tiers, cols), F32),
            pltpu.VMEM((SWEEPS + 1, 2, rows, cols), F32),
            pltpu.VMEM((rows, cols), F32),
            pltpu.VMEM((SWEEPS + 1, 6, rows, cols), F32),
            dma((10,)),
            dma(()),
            dma(()),
            dma(()),
            dma(()),
            dma(()),
            dma(()),
            dma((2,)),
            dma((SWEEPS + 1, 2)),
        ],
        compiler_params=pltpu.CompilerParams(
            collective_id=0, has_side_effects=True, vmem_limit_bytes=VMEM_BYTES
        ),
    )(
        *(
            pltpu.with_memory_space_constraint(given, pltpu.HBM)
            for given in (temp, cond, mass, dyn, leak, panel.reshape(1, slots), place, block, tier, sens)
        )
    )
    return pl.pallas_call(
        hand_over,
        out_shape=(jax.ShapeDtypeStruct(grid, F32),) * 2,
        in_specs=[vmem_spec] * 2,
        out_specs=(any_spec, any_spec),
        scratch_shapes=[dma((2,))],
        compiler_params=pltpu.CompilerParams(vmem_limit_bytes=VMEM_BYTES),
    )(new, power.reshape(grid))


def solution(mesh):
    sizes = (mesh.shape["row"], mesh.shape["col"], mesh.shape["layer"])
    owner = ("row", "col", "layer")
    return jax.shard_map(
        functools.partial(shards, sizes),
        mesh=mesh,
        in_specs=(P("layer", "row", "col"),) * 3
        + (P(owner, None, None),) * 3
        + (P(owner, None),) * 4,
        out_specs=(P("layer", "row", "col"), P("layer", "row", "col")),
        check_vma=False,
    )
```

time: 33.9 us -> 31.9 us (0.941)
  Pallas kernels: 33.1 us -> 31.1 us
    pallas_call x1, Pallas kernels: 32.3 us -> 30.3 us  [shards(): pl.pallas_call(functools.partial(kernel, sizes), out_shape=(pltpu.VMEM(gr...]
where the time goes in v1:
time: 31.9 us; the launch traced here: 31.7 us
  Pallas kernels  31.1 us (97%)
  between operations  0.64 us (2%)
    pallas_call x1, Pallas kernels, shards(): pl.pallas_call(functools.partial(kernel, sizes), out_shape=(pltpu.VMEM(gr...  30.3 us
    pallas_call x1, Pallas kernels, shards(): pl.pallas_call(hand_over, out_shape=(jax.ShapeDtypeStruct(grid, F32),) *...  0.81 us

profile of v1, /device:TPU:0, one launch (start us, length us, event | category | flops | bytes accessed | tf_op | source)
XLA Modules:
  0.0 31.7 jit_solution(10489741590702761545)
XLA Ops:
  0.6 30.3 %shard_map.113 = (f32[4,128,128]{2,1,0:T(8,128)S(1)}, f32[512,128]{1,0:T(8,128)S(1)}) custom-call(f32[4,128,128]{2,1,0:T(8,128)} %temp_hbm.1, f32[4,128,128]{2,1,0:T(8,128)} %cond_hbm.1, f32[4,128,128]{2,1,0:T(8,128)} %mass_hbm.1, bf16[1,64,4096]{2,1,0:T(8,128)(2,1)} %dyn_hbm.1, bf16[1,64,4096]{2,1,0:T(8,128)(2,1)} %leak_hbm.1, s32[1,64]{1,0:T(1,128)} %bitcast.3, ...), custom_call_target="tpu_custom_call" | custom-call | tf_op jit(solution)/shard_map/pallas_call | solution.py:536
  30.9 0.8 %shard_map.114 = (f32[4,128,128]{2,1,0:T(8,128)}, f32[4,128,128]{2,1,0:T(8,128)}) custom-call(f32[4,128,128]{2,1,0:T(8,128)S(1)} %get-tuple-element.4.new, f32[4,128,128]{2,1,0:T(8,128)S(1)} %bitcast.2), custom_call_target="tpu_custom_call" | custom-call | tf_op jit(solution)/shard_map/pallas_call | solution.py:593

commit v2 on v1

--- a/solution.py
+++ b/solution.py
@@ -88,9 +88,16 @@
     resid,
     edge_send,
     edge_recv,
+    edge_spare,
     plane_recv,
+    plane_spare,
+    rim_send,
+    rim_recv,
+    rim_spare,
+    gain_send,
+    gain_recv,
+    gain_spare,
     nothing,
-    waste,
     in_sem,
     note_ssem,
     note_rsem,
@@ -100,6 +107,10 @@
     load_rsem,
     halo_ssem,
     halo_rsem,
+    rim_ssem,
+    rim_rsem,
+    gain_ssem,
+    gain_rsem,
 ):
     n_row, n_col, n_layer = sizes
     tiles = n_row * n_col
@@ -163,6 +174,26 @@
         (my_col < n_col - 1, {"col": my_col + 1}, 5),
     )
 
+    def neighbour(d_row, d_col, d_layer):
+        exists, where = [], {}
+        for axis, mine, count, d in (
+            ("row", my_row, n_row, d_row),
+            ("col", my_col, n_col, d_col),
+            ("layer", my_layer, n_layer, d_layer),
+        ):
+            if d:
+                exists.append(mine > 0 if d < 0 else mine < count - 1)
+                where[axis] = mine + d
+        return functools.reduce(jnp.logical_and, exists), where
+
+    rims_of = (
+        [((a, b, 0), 0, 1, 8 + i) for i, (a, b) in enumerate(((-1, -1), (-1, 1), (1, -1), (1, 1)))]
+        + [((a, 0, c), 0, 1, 12 + i) for i, (a, c) in enumerate(((-1, -1), (-1, 1), (1, -1), (1, 1)))]
+        + [((0, b, c), 2, 1, 16 + i) for i, (b, c) in enumerate(((-1, -1), (-1, 1), (1, -1), (1, 1)))]
+        + [((-1, 0, 0), 0, 2, 0), ((1, 0, 0), 0, 2, 2), ((0, -1, 0), 2, 2, 4), ((0, 1, 0), 2, 2, 6)]
+    )
+    slot_of = {step: slot for step, _, _, slot in rims_of}
+
     nothing[...] = jnp.zeros_like(nothing)
     barrier = pltpu.get_barrier_semaphore()
 
@@ -170,7 +201,8 @@
         lambda other: pl.semaphore_signal(barrier, inc=1, device_id=device(other), device_id_type=MESH)
     )
 
-    for exists, where, side in sides[:2]:
+    across = [neighbour(*step) for step, _, _, _ in rims_of if step[2]] + [neighbour(0, 0, -1), neighbour(0, 0, 1)]
+    for exists, where in across:
 
         @pl.when(exists)
         def _(where=where):
@@ -198,6 +230,11 @@
     def load_copy(other):
         return remote(load_send.at[other], load_recv.at[me], load_ssem, load_rsem, other)
 
+    def send(src, dst, ssem, rsem, where):
+        pltpu.make_async_remote_copy(
+            src_ref=src, dst_ref=dst, send_sem=ssem, recv_sem=rsem, device_id=where, device_id_type=MESH
+        ).start()
+
     def bytes_of(ref, sem):
         return pltpu.make_async_copy(ref, ref, sem)
 
@@ -224,11 +261,42 @@
         )
     means = means * (1.0 / (SUB * SUB))
     note_send[...] = means
-    beyond = (my_layer > 0).astype(jnp.int32) + (my_layer < n_layer - 1).astype(jnp.int32)
+    beyond = sum(exists.astype(jnp.int32) for exists, _ in across)
     pl.semaphore_wait(barrier, tiles - 1 + beyond)
 
     each_peer(lambda other: note_copy(other).start())
     keep(note_send, note_recv.at[me], note_rsem)
+
+    def missing(exists, blocks):
+        @pl.when(jnp.logical_not(exists))
+        def _():
+            for recv, spare, at, ssem, rsem, none in blocks:
+                keep(none, recv.at[at], rsem)
+                keep(none, spare.at[at], ssem)
+
+    none8 = nothing.at[:8, :]
+    for exists, _, side in sides[:2]:
+        missing(
+            exists,
+            [
+                (plane_recv.at[turn], plane_spare.at[turn], side, halo_ssem.at[0], halo_rsem.at[turn, 0], nothing)
+                for turn in range(4)
+            ],
+        )
+    for exists, _, side in sides[2:]:
+        missing(
+            exists,
+            [
+                (edge_recv.at[turn], edge_spare.at[turn], side - 2, halo_ssem.at[1], halo_rsem.at[turn, 1], none8)
+                for turn in range(2)
+            ]
+            + [(gain_recv, gain_spare, 3 * (side - 2) + k, gain_ssem, gain_rsem, none8) for k in range(3)],
+        )
+    for step, _, count, slot in rims_of:
+        missing(
+            neighbour(*step)[0],
+            [(rim_recv, rim_spare, slot + k, rim_ssem, rim_rsem, none8) for k in range(count)],
+        )
     lane_s = iota((slots, slots), 1)
     sub_s = iota((slots, slots), 0)
     eye = lane_s == sub_s
@@ -274,23 +342,7 @@
         @pl.when(exists)
         def _():
             src, dst, kind = halo_ends(turn, field, side, side ^ 1)
-            pltpu.make_async_remote_copy(
-                src_ref=src,
-                dst_ref=dst,
-                send_sem=halo_ssem.at[kind],
-                recv_sem=halo_rsem.at[turn, kind],
-                device_id=where,
-                device_id_type=MESH,
-            ).start()
-
-        @pl.when(jnp.logical_not(exists))
-        def _():
-            _, dst, kind = halo_ends(turn, field, side, side)
-            none = nothing.at[...] if kind == 0 else nothing.at[: 2 * tiers, :]
-            spare = waste.at[turn, side]
-            spare = spare if kind == 0 else spare.at[: 2 * tiers, :]
-            keep(none, dst, halo_rsem.at[turn, kind])
-            keep(none, spare, halo_ssem.at[kind])
+            send(src, dst, halo_ssem.at[kind], halo_rsem.at[turn, kind], where)
 
     def pack_rows(turn, field):
         for end in range(2):
@@ -298,13 +350,16 @@
             for t in range(tiers):
                 edge_send[turn, 0, end * tiers + t : end * tiers + t + 1, :] = field[t, at : at + 1, :]
 
-    def pack_columns(turn, field):
+    def columns_of(field):
         columns = jnp.zeros((2 * tiers, rows), F32)
         for t in range(tiers):
             columns = columns + lax.dot_general(
-                picks[t], two_parts(field[t], 1), (((1,), (1,)), ((), ())), preferred_element_type=F32
+                picks[t], two_parts(field(t), 1), (((1,), (1,)), ((), ())), preferred_element_type=F32
             )
-        edge_send[turn, 1] = columns
+        return columns
+
+    def rows_of(first, last):
+        return jnp.concatenate([first(t) for t in range(tiers)] + [last(t) for t in range(tiers)], axis=0)
 
     def start_halo(turn, field):
         def start(which):
@@ -314,11 +369,14 @@
         pack_rows(turn, field)
         start(sides[2:4])
         start(sides[:2])
-        pack_columns(turn, field)
+        edge_send[turn, 1] = columns_of(lambda t: field[t])
         start(sides[4:])
 
+    def wait_plane(turn):
+        bytes_of(plane_recv.at[turn], halo_rsem.at[turn, 0]).wait()
+
     def wait_halo(turn):
-        bytes_of(plane_recv.at[turn], halo_rsem.at[turn, 0]).wait()
+        wait_plane(turn)
         bytes_of(edge_recv.at[turn], halo_rsem.at[turn, 1]).wait()
 
     row_i = iota((rows, cols), 0)
@@ -343,8 +401,8 @@
         east = jnp.where(col_i == cols - 1, 0.0, pltpu.roll(v, cols - 1, 1))
         return v, (low, high, north, south, west, east)
 
-    def rims(turn):
-        ends = jnp.concatenate([edge_recv[turn, 2], edge_recv[turn, 3]], axis=0)
+    def rims(west, east):
+        ends = jnp.concatenate([west, east], axis=0)
         return lax.dot_general(
             two_parts(ends, 0), put, (((0,), (0,)), ((), ())), preferred_element_type=F32
         )
@@ -358,7 +416,7 @@
         return value
 
     def add_beyond(turn):
-        rim = rims(turn)
+        rim = rims(edge_recv[turn, 2], edge_recv[turn, 3])
         resid[0] = resid[0] + faces[0, 0] * plane_recv[turn, 0]
         resid[tiers - 1] = resid[tiers - 1] + faces[1, tiers - 1] * plane_recv[turn, 1]
         for t in range(tiers):
@@ -437,7 +495,7 @@
     loads[9].wait()
     wait_halo(0)
     wait_halo(1)
-    rim = rims(1)
+    rim = rims(edge_recv[1, 2], edge_recv[1, 3])
     for t in range(tiers):
         c, (low, high, north, south, west, east) = inside(cond, t)
         here = rim[:, t * cols : (t + 1) * cols]
@@ -461,7 +519,43 @@
     middle = (EIG_LOW + EIG_HIGH) / 2.0
     spread = (EIG_HIGH - EIG_LOW) / 2.0
     ratio = middle / spread
-    weight = 1.0 / ratio
+    weight_a = 1.0 / ratio
+    weight_b = 1.0 / (2.0 * ratio - weight_a)
+    weight_c = 1.0 / (2.0 * ratio - weight_b)
+    keep_b, push_b = weight_b * weight_a, 2.0 * weight_b / spread
+    keep_c, push_c = weight_c * weight_b, 2.0 * weight_c / spread
+
+    for t in range(tiers):
+        scaled = push_b * inv[t]
+        for k in range(6):
+            faces[k, t] = scaled * faces[k, t]
+
+    def layer_face(t):
+        if t == 0 and t == tiers - 1:
+            raise ValueError("one tier")
+        return faces[0, t] if t == 0 else faces[1, t] if t == tiers - 1 else jnp.zeros((rows, cols), F32)
+
+    first, last = slice(0, 1), slice(rows - 1, rows)
+    side_face = [jnp.where(col_i == 0, faces[4, t], jnp.where(col_i == cols - 1, faces[5, t], 0.0)) for t in range(tiers)]
+    ends_face = [jnp.where(row_i == 0, faces[2, t], jnp.where(row_i == rows - 1, faces[3, t], 0.0)) for t in range(tiers)]
+    gain_send[0] = rows_of(lambda t: faces[2, t, first, :], lambda t: faces[3, t, last, :])
+    gain_send[1] = rows_of(lambda t: layer_face(t)[first, :], lambda t: layer_face(t)[last, :])
+    gain_send[2] = rows_of(lambda t: side_face[t][first, :], lambda t: side_face[t][last, :])
+    gain_send[3] = columns_of(lambda t: side_face[t])
+    gain_send[4] = columns_of(layer_face)
+    gain_send[5] = columns_of(lambda t: ends_face[t])
+    for exists, where, side in sides[2:]:
+        lands = (side - 2) ^ 1
+
+        @pl.when(exists)
+        def _(where=where, side=side, lands=lands):
+            send(
+                gain_send.at[0:3] if side < 4 else gain_send.at[3:6],
+                gain_recv.at[3 * lands : 3 * lands + 3],
+                gain_ssem,
+                gain_rsem,
+                where,
+            )
 
     sources = tiles * CAP * FOLDS
     sel_i = iota((FOLDS * patches, sources), 0)
@@ -492,26 +586,143 @@
         r = resid[t] + power_ref[t * rows : (t + 1) * rows, :]
         resid[t] = r
         dirs[0, t] = r * inv[t] * (1.0 / middle)
-    for sweep in range(1, SWEEPS):
-        field = dirs.at[sweep - 1]
-        turn = 1 + sweep
-        start_halo(turn, field)
-        weight_new = 1.0 / (2.0 * ratio - weight)
-        for t in range(tiers):
-            base = temp[t] if sweep == 1 else out_ref[t]
-            out_ref[t] = base + field[t]
-            resid[t] = resid[t] - apply_inside(field, t)
-        wait_halo(turn)
-        add_beyond(turn)
-        for t in range(tiers):
-            d = weight_new * weight * field[t] + (2.0 * weight_new / spread) * (resid[t] * inv[t])
-            if sweep < SWEEPS - 1:
-                dirs[sweep, t] = d
-            else:
-                out_ref[t] = out_ref[t] + d
-        weight = weight_new
+    start, after = dirs.at[0], dirs.at[1]
+
+    def send_rims(which):
+        for step, block, count, _ in which:
+            exists, where = neighbour(*step)
+            lands = slot_of[tuple(-d for d in step)]
+
+            @pl.when(exists)
+            def _(where=where, block=block, count=count, lands=lands):
+                send(
+                    rim_send.at[block : block + count],
+                    rim_recv.at[lands : lands + count],
+                    rim_ssem,
+                    rim_rsem,
+                    where,
+                )
+
+    def send_planes(turn, field):
+        for exists, where, side in sides[:2]:
+            halo_start(turn, field, exists, where, side)
+
+    def around_sum(field, t):
+        v, around = inside(field, t)
+        value = None
+        for k in range(6):
+            if not (k == 0 and t == 0 or k == 1 and t == tiers - 1):
+                term = faces[k, t] * around[k]
+                value = term if value is None else value + term
+        return v, value
+
+    own_rows = rows_of(lambda t: start[t, first, :], lambda t: start[t, last, :])
+    rim_send[0] = own_rows
+    send_rims(rims_of[:8])
+    own_columns = columns_of(lambda t: start[t])
+    rim_send[2] = own_columns
+    send_rims(rims_of[8:12])
+    stay = keep_b + push_b * (middle - 1.0)
+    for t in range(tiers):
+        v, value = around_sum(start, t)
+        after[t] = stay * v + value
+    rim_send[1] = rows_of(lambda t: after[t, first, :], lambda t: after[t, last, :])
+    send_rims(rims_of[12:14])
+    rim_send[3] = columns_of(lambda t: after[t])
+    send_rims(rims_of[14:])
+    send_planes(2, start)
+    bytes_of(gain_recv, gain_rsem).wait()
+    wait_plane(2)
+    bytes_of(rim_recv, rim_rsem).wait()
+
+    eight_s = iota((2 * tiers, cols), 0)
+    eight_l = iota((2 * tiers, cols), 1)
+    upper = eight_s >= tiers
+    tier_s = mod(eight_s, tiers)
+
+    def pair(a, b):
+        return jnp.where(upper, a, b)
+
+    def swap(x):
+        return pltpu.roll(x, tiers, 0)
+
+    def layer_part(down, up):
+        return jnp.where(
+            tier_s == 0, pltpu.roll(down, tiers + 1, 0), jnp.where(tier_s == tiers - 1, pltpu.roll(up, tiers - 1, 0), 0.0)
+        )
+
+    north_west, north_east, south_west, south_east = (rim_recv[8 + i] for i in range(4))
+
+    def shell(own, at, layer_at, gain_at, side_part):
+        return (
+            pair(rim_recv[at + 1], rim_recv[at + 3])
+            + pair(gain_recv[gain_at], gain_recv[gain_at + 3]) * swap(own)
+            + pair(gain_recv[gain_at + 1], gain_recv[gain_at + 4])
+            * layer_part(
+                pair(rim_recv[layer_at], rim_recv[layer_at + 2]), pair(rim_recv[layer_at + 1], rim_recv[layer_at + 3])
+            )
+            + pair(gain_recv[gain_at + 2], gain_recv[gain_at + 5]) * side_part
+        )
+
+    row_shell = shell(
+        own_rows,
+        0,
+        12,
+        0,
+        jnp.where(
+            eight_l == 0,
+            pltpu.roll(pair(north_west, south_west), 1, 1),
+            pltpu.roll(pair(north_east, south_east), cols - 1, 1),
+        ),
+    )
+    col_shell = shell(
+        own_columns,
+        4,
+        16,
+        6,
+        jnp.where(
+            eight_l == 0,
+            pair(pltpu.roll(north_west, 1, 1), swap(north_east)),
+            pair(swap(south_west), pltpu.roll(south_east, cols - 1, 1)),
+        ),
+    )
+    rim_a = rims(rim_recv[4], rim_recv[6])
+    rim_b = rims(col_shell, col_shell)
+
+    def beyond_rows(ref, t, scale, north, south, rim):
+        ref[t, first, :] = ref[t, first, :] + scale * faces[2, t, first, :] * north
+        ref[t, last, :] = ref[t, last, :] + scale * faces[3, t, last, :] * south
+        face = jnp.where(col_i == 0, faces[4, t], faces[5, t])
+        ref[t] = ref[t] + scale * face * rim[:, t * cols : (t + 1) * cols]
+
+    outer = sorted(range(tiers), key=lambda t: 0 < t < tiers - 1)
+    for t in outer:
+        if t == 0:
+            after[t] = after[t] + faces[0, t] * plane_recv[2, 0]
+        if t == tiers - 1:
+            after[t] = after[t] + faces[1, t] * plane_recv[2, 1]
+        beyond_rows(
+            after, t, 1.0, rim_recv[0, tiers + t : tiers + t + 1, :], rim_recv[2, t : t + 1, :], rim_a
+        )
+        if t == outer[min(1, tiers - 1)]:
+            send_planes(3, after)
+    lift = push_c / push_b
+    old = 1.0 - lift * keep_b
+    now = 1.0 + keep_c + lift - push_c
+    for t in range(tiers):
+        v, value = around_sum(after, t)
+        out_ref[t] = temp[t] + old * start[t] + now * v + lift * value
+        beyond_rows(
+            out_ref, t, lift, row_shell[tiers + t : tiers + t + 1, :], row_shell[t : t + 1, :], rim_b
+        )
+    wait_plane(3)
+    out_ref[0] = out_ref[0] + lift * faces[0, 0] * plane_recv[3, 0]
+    out_ref[tiers - 1] = out_ref[tiers - 1] + lift * faces[1, tiers - 1] * plane_recv[3, 1]
+
     bytes_of(plane_recv, halo_ssem.at[0]).wait()
     bytes_of(edge_recv, halo_ssem.at[1]).wait()
+    bytes_of(rim_recv, rim_ssem).wait()
+    bytes_of(gain_recv, gain_ssem).wait()
     bytes_of(note_recv.at[1:], note_ssem).wait()
     bytes_of(place_recv.at[8:, :], place_ssem).wait()
     bytes_of(load_recv.at[1:], load_ssem).wait()
@@ -566,11 +777,18 @@
             pltpu.VMEM(grid, F32),
             pltpu.VMEM(grid, F32),
             pltpu.VMEM(grid, F32),
-            pltpu.VMEM((SWEEPS + 1, 2, 2 * tiers, cols), F32),
-            pltpu.VMEM((SWEEPS + 1, 4, 2 * tiers, cols), F32),
-            pltpu.VMEM((SWEEPS + 1, 2, rows, cols), F32),
+            pltpu.VMEM((2, 2, 2 * tiers, cols), F32),
+            pltpu.VMEM((2, 4, 2 * tiers, cols), F32),
+            pltpu.VMEM((2, 4, 2 * tiers, cols), F32),
+            pltpu.VMEM((4, 2, rows, cols), F32),
+            pltpu.VMEM((4, 2, rows, cols), F32),
+            pltpu.VMEM((4, 2 * tiers, cols), F32),
+            pltpu.VMEM((20, 2 * tiers, cols), F32),
+            pltpu.VMEM((20, 2 * tiers, cols), F32),
+            pltpu.VMEM((6, 2 * tiers, cols), F32),
+            pltpu.VMEM((12, 2 * tiers, cols), F32),
+            pltpu.VMEM((12, 2 * tiers, cols), F32),
             pltpu.VMEM((rows, cols), F32),
-            pltpu.VMEM((SWEEPS + 1, 6, rows, cols), F32),
             dma((10,)),
             dma(()),
             dma(()),
@@ -579,7 +797,11 @@
             dma(()),
             dma(()),
             dma((2,)),
-            dma((SWEEPS + 1, 2)),
+            dma((4, 2)),
+            dma(()),
+            dma(()),
+            dma(()),
+            dma(()),
         ],
         compiler_params=pltpu.CompilerParams(
             collective_id=0, has_side_effects=True, vmem_limit_bytes=VMEM_BYTES

time: 31.9 us -> 30 us (0.940)
  Pallas kernels: 31.1 us -> 29.2 us
    pallas_call x1, Pallas kernels: 30.3 us -> 28.4 us  [shards(): pl.pallas_call(functools.partial(kernel, sizes), out_shape=(pltpu.VMEM(gr...]
where the time goes in v2:
time: 30 us; the launch traced here: 29.9 us
  Pallas kernels  29.2 us (97%)
  between operations  0.64 us (2%)
    pallas_call x1, Pallas kernels, shards(): pl.pallas_call(functools.partial(kernel, sizes), out_shape=(pltpu.VMEM(gr...  28.4 us
    pallas_call x1, Pallas kernels, shards(): pl.pallas_call(hand_over, out_shape=(jax.ShapeDtypeStruct(grid, F32),) *...  0.81 us

profile of v2, /device:TPU:0, one launch (start us, length us, event | category | flops | bytes accessed | tf_op | source)
XLA Modules:
  0.0 29.9 jit_solution(3556342616476477526)
XLA Ops:
  0.6 28.4 %shard_map.113 = (f32[4,128,128]{2,1,0:T(8,128)S(1)}, f32[512,128]{1,0:T(8,128)S(1)}) custom-call(f32[4,128,128]{2,1,0:T(8,128)} %temp_hbm.1, f32[4,128,128]{2,1,0:T(8,128)} %cond_hbm.1, f32[4,128,128]{2,1,0:T(8,128)} %mass_hbm.1, bf16[1,64,4096]{2,1,0:T(8,128)(2,1)} %dyn_hbm.1, bf16[1,64,4096]{2,1,0:T(8,128)(2,1)} %leak_hbm.1, s32[1,64]{1,0:T(1,128)} %bitcast.3, ...), custom_call_target="tpu_custom_call" | custom-call | tf_op jit(solution)/shard_map/pallas_call | solution.py:747
  29.1 0.8 %shard_map.114 = (f32[4,128,128]{2,1,0:T(8,128)}, f32[4,128,128]{2,1,0:T(8,128)}) custom-call(f32[4,128,128]{2,1,0:T(8,128)S(1)} %get-tuple-element.4.new, f32[4,128,128]{2,1,0:T(8,128)S(1)} %bitcast.2), custom_call_target="tpu_custom_call" | custom-call | tf_op jit(solution)/shard_map/pallas_call | solution.py:815

commit v3 on v2

--- a/solution.py
+++ b/solution.py
@@ -12,7 +12,8 @@
 EIG_LOW = 0.1
 EIG_HIGH = 2.0
 LANES = 128
-FOLDS = 16
+FOLDS = 4
+EARLY = 1
 VMEM_BYTES = 40 << 20
 
 MESH = pl.DeviceIdType.MESH
@@ -79,6 +80,11 @@
     place_send,
     place_recv,
     fac,
+    fac_send,
+    fac_recv,
+    early_send,
+    early_recv,
+    early_power,
     load_send,
     load_recv,
     dirs,
@@ -103,6 +109,10 @@
     note_rsem,
     place_ssem,
     place_rsem,
+    fac_ssem,
+    fac_rsem,
+    early_ssem,
+    early_rsem,
     load_ssem,
     load_rsem,
     halo_ssem,
@@ -118,6 +128,7 @@
     slots, cells = dyn.shape
     wide = cells // FOLDS
     halves = wide // LANES
+    rows_of_tile = CAP * FOLDS
     named = 8 * tiles
     in_plane = (rows // SUB) * (cols // SUB)
     patches = tiers * in_plane
@@ -218,14 +229,17 @@
             device_id_type=MESH,
         )
 
-    def eight(tile):
-        return pl.ds(pl.multiple_of(tile * 8, 8), 8)
-
     def note_copy(other):
         return remote(note_send, note_recv.at[me], note_ssem, note_rsem, other)
 
     def place_copy(other):
-        return remote(place_send.at[eight(other), :], place_recv.at[eight(me), :], place_ssem, place_rsem, other)
+        return remote(place_send.at[other], place_recv.at[me], place_ssem, place_rsem, other)
+
+    def fac_copy(other):
+        return remote(fac_send.at[other], fac_recv.at[me], fac_ssem, fac_rsem, other)
+
+    def early_copy(other):
+        return remote(early_send.at[other], early_recv.at[me], early_ssem, early_rsem, other)
 
     def load_copy(other):
         return remote(load_send.at[other], load_recv.at[me], load_ssem, load_rsem, other)
@@ -261,42 +275,6 @@
         )
     means = means * (1.0 / (SUB * SUB))
     note_send[...] = means
-    beyond = sum(exists.astype(jnp.int32) for exists, _ in across)
-    pl.semaphore_wait(barrier, tiles - 1 + beyond)
-
-    each_peer(lambda other: note_copy(other).start())
-    keep(note_send, note_recv.at[me], note_rsem)
-
-    def missing(exists, blocks):
-        @pl.when(jnp.logical_not(exists))
-        def _():
-            for recv, spare, at, ssem, rsem, none in blocks:
-                keep(none, recv.at[at], rsem)
-                keep(none, spare.at[at], ssem)
-
-    none8 = nothing.at[:8, :]
-    for exists, _, side in sides[:2]:
-        missing(
-            exists,
-            [
-                (plane_recv.at[turn], plane_spare.at[turn], side, halo_ssem.at[0], halo_rsem.at[turn, 0], nothing)
-                for turn in range(4)
-            ],
-        )
-    for exists, _, side in sides[2:]:
-        missing(
-            exists,
-            [
-                (edge_recv.at[turn], edge_spare.at[turn], side - 2, halo_ssem.at[1], halo_rsem.at[turn, 1], none8)
-                for turn in range(2)
-            ]
-            + [(gain_recv, gain_spare, 3 * (side - 2) + k, gain_ssem, gain_rsem, none8) for k in range(3)],
-        )
-    for step, _, count, slot in rims_of:
-        missing(
-            neighbour(*step)[0],
-            [(rim_recv, rim_spare, slot + k, rim_ssem, rim_rsem, none8) for k in range(count)],
-        )
     lane_s = iota((slots, slots), 1)
     sub_s = iota((slots, slots), 0)
     eye = lane_s == sub_s
@@ -324,6 +302,29 @@
     pos_col = tier_col * in_plane + sub_col
     goes = (tgt_row * CAP + rank_row) == iota((tiles * CAP, slots), 0).astype(F32)
     pick = jnp.where(goes, 1.0, 0.0).astype(BF16)
+    loads[6].wait()
+    loads[7].wait()
+    for src, dst in ((dyn, dyn_pick), (leak, leak_pick)):
+        for fold in range(FOLDS):
+            taken = jnp.dot(pick, src[:, fold * wide : (fold + 1) * wide], preferred_element_type=F32)
+            for half in range(halves):
+                dst[half, pl.ds(fold, tiles * CAP, stride=FOLDS), :] = taken[
+                    :, half * LANES : (half + 1) * LANES
+                ]
+    for tile in range(tiles):
+        for half in range(EARLY):
+            at, lanes = slice(tile * rows_of_tile, (tile + 1) * rows_of_tile), slice(half * LANES, (half + 1) * LANES)
+            early_send[tile, 0, :, lanes] = dyn_pick[half, at, :].astype(BF16)
+            early_send[tile, 1, :, lanes] = leak_pick[half, at, :].astype(BF16)
+
+    beyond = sum(exists.astype(jnp.int32) for exists, _ in across)
+    pl.semaphore_wait(barrier, tiles - 1 + beyond)
+
+    each_peer(lambda other: note_copy(other).start())
+    keep(note_send, note_recv.at[me], note_rsem)
+    each_peer(lambda other: early_copy(other).start())
+    keep(early_send.at[me], early_recv.at[me], early_rsem)
+
     sub8 = iota((2 * tiers, 2 * cols), 0)
     lane8 = mod(iota((2 * tiers, 2 * cols), 1), cols)
     picks = [
@@ -448,23 +449,19 @@
     block_size = jnp.maximum(jnp.sum(same_block, axis=1, keepdims=True), 1.0)
     same_three = jnp.concatenate([same_block.astype(BF16)] * 3, axis=1)
     at_place = (iota((named, LANES), 1) + 1).astype(F32) == pos_r
-    place_send[...] = jnp.broadcast_to(pos_r, place_send.shape)
+    group = div(iota((8, LANES), 1), LANES // CAP) == iota((8, LANES), 0)
+
+    def one_row(block):
+        return jnp.sum(jnp.where(group, block, 0.0), axis=0, keepdims=True)
+
+    for tile in range(tiles):
+        place_send[tile] = one_row(jnp.broadcast_to(pos_r[tile * 8 : (tile + 1) * 8], (8, LANES)))
     each_peer(lambda other: place_copy(other).start())
-    keep(place_send.at[eight(me), :], place_recv.at[eight(me), :], place_rsem)
+    keep(place_send.at[me], place_recv.at[me], place_rsem)
 
     loads[8].wait()
     start_halo(0, temp)
     start_halo(1, cond)
-
-    loads[6].wait()
-    loads[7].wait()
-    for src, dst in ((dyn, dyn_pick), (leak, leak_pick)):
-        for fold in range(FOLDS):
-            taken = jnp.dot(pick, src[:, fold * wide : (fold + 1) * wide], preferred_element_type=F32)
-            for half in range(halves):
-                dst[half, pl.ds(fold, tiles * CAP, stride=FOLDS), :] = taken[
-                    :, half * LANES : (half + 1) * LANES
-                ]
 
     bytes_of(note_recv, note_rsem).wait()
     tile_means = jnp.concatenate([jnp.broadcast_to(note_recv[tile], (8, LANES)) for tile in range(tiles)], axis=0)
@@ -474,24 +471,64 @@
     )
     fac[...] = jnp.broadcast_to(jnp.exp(sens_r * (block_sum / block_size)), (named, LANES))
 
+    upper_rank = iota((8, LANES), 0) >= FOLDS
+    for tile in range(tiles):
+        fac_send[tile] = one_row(fac[tile * 8 : (tile + 1) * 8, :])
+    each_peer(lambda other: fac_copy(other).start())
+    keep(fac_send.at[me], fac_recv.at[me], fac_rsem)
+
+
     @pl.loop(0, tiles)
     def _(step):
         other = far_first(step)
-        for rank in range(CAP):
-            by = fac[pl.ds(other * 8 + rank, 8, stride=0), :]
-            by = jnp.concatenate([by] * (FOLDS // 8), axis=0)
-            at = pl.ds(pl.multiple_of((other * CAP + rank) * FOLDS, FOLDS), FOLDS)
-            for half in range(halves):
-                load_send[other, rank * FOLDS : (rank + 1) * FOLDS, half * LANES : (half + 1) * LANES] = (
-                    dyn_pick[half, at, :] + by * leak_pick[half, at, :]
-                ).astype(BF16)
+
+        def factor_of(rank):
+            return fac[pl.ds(other * 8 + rank, 8, stride=0), :]
+
+        by = jnp.concatenate(
+            [jnp.where(upper_rank, factor_of(rank + 1), factor_of(rank)) for rank in range(0, CAP, 2)], axis=0
+        )
+        at = pl.ds(pl.multiple_of(other * rows_of_tile, rows_of_tile), rows_of_tile)
+        for half in range(EARLY, halves):
+            load_send[other, :, (half - EARLY) * LANES : (half - EARLY + 1) * LANES] = (
+                dyn_pick[half, at, :] + by * leak_pick[half, at, :]
+            ).astype(BF16)
 
         @pl.when(other != me)
         def _():
             load_copy(other).start()
 
     keep(load_send.at[me], load_recv.at[me], load_rsem)
-
+    def missing(exists, blocks):
+        @pl.when(jnp.logical_not(exists))
+        def _():
+            for recv, spare, at, ssem, rsem, none in blocks:
+                keep(none, recv.at[at], rsem)
+                keep(none, spare.at[at], ssem)
+
+    none8 = nothing.at[:8, :]
+    for exists, _, side in sides[:2]:
+        missing(
+            exists,
+            [
+                (plane_recv.at[turn], plane_spare.at[turn], side, halo_ssem.at[0], halo_rsem.at[turn, 0], nothing)
+                for turn in range(4)
+            ],
+        )
+    for exists, _, side in sides[2:]:
+        missing(
+            exists,
+            [
+                (edge_recv.at[turn], edge_spare.at[turn], side - 2, halo_ssem.at[1], halo_rsem.at[turn, 1], none8)
+                for turn in range(2)
+            ]
+            + [(gain_recv, gain_spare, 3 * (side - 2) + k, gain_ssem, gain_rsem, none8) for k in range(3)],
+        )
+    for step, _, count, slot in rims_of:
+        missing(
+            neighbour(*step)[0],
+            [(rim_recv, rim_spare, slot + k, rim_ssem, rim_rsem, none8) for k in range(count)],
+        )
     loads[9].wait()
     wait_halo(0)
     wait_halo(1)
@@ -564,24 +601,41 @@
     sel_patch = mod(sel_in, bands) * per_band + div(sel_in, bands)
     fold_hit = div(sel_i, patches) == mod(sel_j, FOLDS)
     bytes_of(place_recv, place_rsem).wait()
-    place_i = iota((named, sources), 0)
-    place_j = div(iota((named, sources), 1), FOLDS)
-    place_j = div(place_j, CAP) * 8 + mod(place_j, CAP)
-    places = jnp.concatenate([place_recv[...]] * (sources // LANES), axis=1)
-    code = jnp.sum(jnp.where(place_i == place_j, places, 0.0), axis=0, keepdims=True)
+    def by_source(ref):
+        taken = jnp.concatenate([jnp.broadcast_to(ref[tile], (rows_of_tile, LANES)) for tile in range(tiles)], axis=0)
+        rank = div(mod(iota(taken.shape, 0), rows_of_tile), FOLDS)
+        return jnp.sum(jnp.where(iota(taken.shape, 1) == rank * (LANES // CAP), taken, 0.0), axis=1, keepdims=True)
+
+    same = iota((sources, sources), 0) == iota((sources, sources), 1)
+    code = jnp.sum(jnp.where(same, by_source(place_recv), 0.0), axis=0, keepdims=True)
     picker = jnp.where(fold_hit & (code == (sel_patch + 1).astype(F32)), 1.0, 0.0).astype(BF16)
+    left = iota((bands, LANES), 1) < SUB
+
+    def deposit(footprint, begin, end):
+        for fold in range(FOLDS):
+            for k in range(begin, end):
+                lanes = slice((k - begin) * LANES, (k - begin + 1) * LANES)
+                a = footprint[fold * patches : fold * patches + bands, lanes]
+                b = footprint[fold * patches + bands : fold * patches + 2 * bands, lanes]
+                at = 2 * (fold * halves + k)
+                power_ref[pl.ds(at, bands, stride=SUB), :] = jnp.where(left, a, pltpu.roll(b, SUB, 1))
+                power_ref[pl.ds(at + 1, bands, stride=SUB), :] = jnp.where(left, pltpu.roll(a, SUB, 1), b)
+
+    bytes_of(fac_recv, fac_rsem).wait()
+    factors = by_source(fac_recv)
+    bytes_of(early_recv, early_rsem).wait()
+    for half in range(EARLY):
+        lanes = slice(half * LANES, (half + 1) * LANES)
+        for tile in range(tiles):
+            early_power[tile * rows_of_tile : (tile + 1) * rows_of_tile, lanes] = (
+                early_recv[tile, 0, :, lanes].astype(F32)
+                + factors[tile * rows_of_tile : (tile + 1) * rows_of_tile] * early_recv[tile, 1, :, lanes].astype(F32)
+            ).astype(BF16)
+    deposit(jnp.dot(picker, early_power[...], preferred_element_type=F32), 0, EARLY)
     bytes_of(load_recv, load_rsem).wait()
-    footprint = jnp.dot(picker, load_recv[...].reshape(sources, wide), preferred_element_type=F32)
-    left = iota((bands, LANES), 1) < SUB
-    for fold in range(FOLDS):
-        for k in range(wide // LANES):
-            lanes = slice(k * LANES, (k + 1) * LANES)
-            a = footprint[fold * patches : fold * patches + bands, lanes]
-            b = footprint[fold * patches + bands : fold * patches + 2 * bands, lanes]
-            at = 2 * (fold * (wide // LANES) + k)
-            power_ref[pl.ds(at, bands, stride=SUB), :] = jnp.where(left, a, pltpu.roll(b, SUB, 1))
-            power_ref[pl.ds(at + 1, bands, stride=SUB), :] = jnp.where(left, pltpu.roll(a, SUB, 1), b)
-
+    deposit(
+        jnp.dot(picker, load_recv[...].reshape(sources, wide - EARLY * LANES), preferred_element_type=F32), EARLY, halves
+    )
     for t in range(tiers):
         r = resid[t] + power_ref[t * rows : (t + 1) * rows, :]
         resid[t] = r
@@ -724,7 +778,9 @@
     bytes_of(rim_recv, rim_ssem).wait()
     bytes_of(gain_recv, gain_ssem).wait()
     bytes_of(note_recv.at[1:], note_ssem).wait()
-    bytes_of(place_recv.at[8:, :], place_ssem).wait()
+    bytes_of(place_recv.at[1:], place_ssem).wait()
+    bytes_of(fac_recv.at[1:], fac_ssem).wait()
+    bytes_of(early_recv.at[1:], early_ssem).wait()
     bytes_of(load_recv.at[1:], load_ssem).wait()
 
 
@@ -767,11 +823,16 @@
             pltpu.VMEM((cells // FOLDS // LANES, tiles * CAP * FOLDS, LANES), F32),
             pltpu.VMEM((1, LANES), F32),
             pltpu.VMEM((tiles, 1, LANES), F32),
+            pltpu.VMEM((tiles, 1, LANES), F32),
+            pltpu.VMEM((tiles, 1, LANES), F32),
             pltpu.VMEM((8 * tiles, LANES), F32),
-            pltpu.VMEM((8 * tiles, LANES), F32),
-            pltpu.VMEM((8 * tiles, LANES), F32),
-            pltpu.VMEM((tiles, CAP * FOLDS, cells // FOLDS), BF16),
-            pltpu.VMEM((tiles, CAP * FOLDS, cells // FOLDS), BF16),
+            pltpu.VMEM((tiles, 1, LANES), F32),
+            pltpu.VMEM((tiles, 1, LANES), F32),
+            pltpu.VMEM((tiles, 2, CAP * FOLDS, EARLY * LANES), BF16),
+            pltpu.VMEM((tiles, 2, CAP * FOLDS, EARLY * LANES), BF16),
+            pltpu.VMEM((tiles * CAP * FOLDS, EARLY * LANES), BF16),
+            pltpu.VMEM((tiles, CAP * FOLDS, cells // FOLDS - EARLY * LANES), BF16),
+            pltpu.VMEM((tiles, CAP * FOLDS, cells // FOLDS - EARLY * LANES), BF16),
             pltpu.VMEM((SWEEPS - 1,) + grid, F32),
             pltpu.VMEM((6,) + grid, F32),
             pltpu.VMEM(grid, F32),
@@ -796,6 +857,10 @@
             dma(()),
             dma(()),
             dma(()),
+            dma(()),
+            dma(()),
+            dma(()),
+            dma(()),
             dma((2,)),
             dma((4, 2)),
             dma(()),

time: 30 us -> 28.9 us (0.963)
  Pallas kernels: 29.2 us -> 28.1 us
    pallas_call x1, Pallas kernels: 28.4 us -> 27.3 us  [shards(): pl.pallas_call(functools.partial(kernel, sizes), out_shape=(pltpu.VMEM(gr...]
where the time goes in v3:
time: 28.9 us; the launch traced here: 28.7 us
  Pallas kernels  28.1 us (97%)
  between operations  0.64 us (2%)
    pallas_call x1, Pallas kernels, shards(): pl.pallas_call(functools.partial(kernel, sizes), out_shape=(pltpu.VMEM(gr...  27.3 us
    pallas_call x1, Pallas kernels, shards(): pl.pallas_call(hand_over, out_shape=(jax.ShapeDtypeStruct(grid, F32),) *...  0.81 us

profile of v3, /device:TPU:0, one launch (start us, length us, event | category | flops | bytes accessed | tf_op | source)
XLA Modules:
  0.0 28.7 jit_solution(5532083211994513537)
XLA Ops:
  0.6 27.3 %shard_map.113 = (f32[4,128,128]{2,1,0:T(8,128)S(1)}, f32[512,128]{1,0:T(8,128)S(1)}) custom-call(f32[4,128,128]{2,1,0:T(8,128)} %temp_hbm.1, f32[4,128,128]{2,1,0:T(8,128)} %cond_hbm.1, f32[4,128,128]{2,1,0:T(8,128)} %mass_hbm.1, bf16[1,64,4096]{2,1,0:T(8,128)(2,1)} %dyn_hbm.1, bf16[1,64,4096]{2,1,0:T(8,128)(2,1)} %leak_hbm.1, s32[1,64]{1,0:T(1,128)} %bitcast.3, ...), custom_call_target="tpu_custom_call" | custom-call | tf_op jit(solution)/shard_map/pallas_call | solution.py:803
  27.9 0.8 %shard_map.114 = (f32[4,128,128]{2,1,0:T(8,128)}, f32[4,128,128]{2,1,0:T(8,128)}) custom-call(f32[4,128,128]{2,1,0:T(8,128)S(1)} %get-tuple-element.4.new, f32[4,128,128]{2,1,0:T(8,128)S(1)} %bitcast.2), custom_call_target="tpu_custom_call" | custom-call | tf_op jit(solution)/shard_map/pallas_call | solution.py:880

commit v4 on v3

--- a/solution.py
+++ b/solution.py
@@ -103,6 +103,9 @@
     gain_send,
     gain_recv,
     gain_spare,
+    face_send,
+    face_recv,
+    face_spare,
     nothing,
     in_sem,
     note_ssem,
@@ -121,6 +124,8 @@
     rim_rsem,
     gain_ssem,
     gain_rsem,
+    face_ssem,
+    face_rsem,
 ):
     n_row, n_col, n_layer = sizes
     tiles = n_row * n_col
@@ -402,10 +407,11 @@
         east = jnp.where(col_i == cols - 1, 0.0, pltpu.roll(v, cols - 1, 1))
         return v, (low, high, north, south, west, east)
 
-    def rims(west, east):
+    def rims(west, east, t=None):
         ends = jnp.concatenate([west, east], axis=0)
+        into = put if t is None else put[:, t * cols : (t + 1) * cols]
         return lax.dot_general(
-            two_parts(ends, 0), put, (((0,), (0,)), ((), ())), preferred_element_type=F32
+            two_parts(ends, 0), into, (((0,), (0,)), ((), ())), preferred_element_type=F32
         )
 
     def apply_inside(field, t):
@@ -513,7 +519,8 @@
             [
                 (plane_recv.at[turn], plane_spare.at[turn], side, halo_ssem.at[0], halo_rsem.at[turn, 0], nothing)
                 for turn in range(4)
-            ],
+            ]
+            + [(face_recv.at[side], face_spare.at[side], k, face_ssem, face_rsem, nothing) for k in range(3)],
         )
     for exists, _, side in sides[2:]:
         missing(
@@ -581,6 +588,16 @@
     gain_send[3] = columns_of(lambda t: side_face[t])
     gain_send[4] = columns_of(layer_face)
     gain_send[5] = columns_of(lambda t: ends_face[t])
+    for exists, where, side in sides[:2]:
+        t = 0 if side == 0 else tiers - 1
+        face_send[side, 0] = faces[side, t]
+        face_send[side, 1] = ends_face[t]
+        face_send[side, 2] = side_face[t]
+
+        @pl.when(exists)
+        def _(where=where, side=side):
+            send(face_send.at[side], face_recv.at[side ^ 1], face_ssem, face_rsem, where)
+
     for exists, where, side in sides[2:]:
         lands = (side - 2) ^ 1
 
@@ -673,21 +690,69 @@
     own_rows = rows_of(lambda t: start[t, first, :], lambda t: start[t, last, :])
     rim_send[0] = own_rows
     send_rims(rims_of[:8])
+    send_planes(2, start)
+    stay = keep_b + push_b * (middle - 1.0)
+    slab_lane = iota((8, cols), 1)
+
+    def slab_row(t, begin, row, inward, shift):
+        slab = slice(begin, begin + 8)
+        v = start[t, slab, :]
+        value = stay * v + faces[inward, t, slab, :] * pltpu.roll(v, shift, 0)
+        value = value + faces[4, t, slab, :] * jnp.where(slab_lane == 0, 0.0, pltpu.roll(v, 1, 1))
+        value = value + faces[5, t, slab, :] * jnp.where(slab_lane == cols - 1, 0.0, pltpu.roll(v, cols - 1, 1))
+        if t > 0:
+            value = value + faces[0, t, slab, :] * start[t - 1, slab, :]
+        if t < tiers - 1:
+            value = value + faces[1, t, slab, :] * start[t + 1, slab, :]
+        return value[row : row + 1, :]
+
+    rim_send[1] = rows_of(lambda t: slab_row(t, 0, 0, 3, 7), lambda t: slab_row(t, rows - 8, 7, 2, 1))
+    send_rims(rims_of[12:14])
     own_columns = columns_of(lambda t: start[t])
     rim_send[2] = own_columns
     send_rims(rims_of[8:12])
-    stay = keep_b + push_b * (middle - 1.0)
     for t in range(tiers):
         v, value = around_sum(start, t)
         after[t] = stay * v + value
-    rim_send[1] = rows_of(lambda t: after[t, first, :], lambda t: after[t, last, :])
-    send_rims(rims_of[12:14])
+    send_planes(3, after)
     rim_send[3] = columns_of(lambda t: after[t])
     send_rims(rims_of[14:])
-    send_planes(2, start)
     bytes_of(gain_recv, gain_rsem).wait()
     wait_plane(2)
+    wait_plane(3)
+    bytes_of(face_recv, face_rsem).wait()
     bytes_of(rim_recv, rim_rsem).wait()
+
+    rim_a = rims(rim_recv[4], rim_recv[6])
+
+    def beyond_rows(ref, t, scale, north, south, rim):
+        ref[t, first, :] = ref[t, first, :] + scale * faces[2, t, first, :] * north
+        ref[t, last, :] = ref[t, last, :] + scale * faces[3, t, last, :] * south
+        face = jnp.where(col_i == 0, faces[4, t], faces[5, t])
+        ref[t] = ref[t] + scale * face * rim[:, t * cols : (t + 1) * cols]
+
+    second = resid
+    for t in range(tiers):
+        value = after[t]
+        if t == 0:
+            value = value + faces[0, t] * plane_recv[2, 0]
+        if t == tiers - 1:
+            value = value + faces[1, t] * plane_recv[2, 1]
+        second[t] = value
+        beyond_rows(
+            second, t, 1.0, rim_recv[0, tiers + t : tiers + t + 1, :], rim_recv[2, t : t + 1, :], rim_a
+        )
+
+    for side, t in ((0, tiers - 1), (1, 0)):
+        plane = plane_recv.at[3, side]
+        rim = rims(rim_recv[16 + side], rim_recv[18 + side], t)
+        plane[...] = (
+            plane[...] + face_recv[side, 0] * start[0 if side == 0 else tiers - 1] + face_recv[side, 2] * rim
+        )
+        plane[first, :] = (
+            plane[first, :] + face_recv[side, 1, first, :] * rim_recv[12 + side, tiers + t : tiers + t + 1, :]
+        )
+        plane[last, :] = plane[last, :] + face_recv[side, 1, last, :] * rim_recv[14 + side, t : t + 1, :]
 
     eight_s = iota((2 * tiers, cols), 0)
     eight_l = iota((2 * tiers, cols), 1)
@@ -740,43 +805,26 @@
             pair(swap(south_west), pltpu.roll(south_east, cols - 1, 1)),
         ),
     )
-    rim_a = rims(rim_recv[4], rim_recv[6])
     rim_b = rims(col_shell, col_shell)
 
-    def beyond_rows(ref, t, scale, north, south, rim):
-        ref[t, first, :] = ref[t, first, :] + scale * faces[2, t, first, :] * north
-        ref[t, last, :] = ref[t, last, :] + scale * faces[3, t, last, :] * south
-        face = jnp.where(col_i == 0, faces[4, t], faces[5, t])
-        ref[t] = ref[t] + scale * face * rim[:, t * cols : (t + 1) * cols]
-
-    outer = sorted(range(tiers), key=lambda t: 0 < t < tiers - 1)
-    for t in outer:
-        if t == 0:
-            after[t] = after[t] + faces[0, t] * plane_recv[2, 0]
-        if t == tiers - 1:
-            after[t] = after[t] + faces[1, t] * plane_recv[2, 1]
-        beyond_rows(
-            after, t, 1.0, rim_recv[0, tiers + t : tiers + t + 1, :], rim_recv[2, t : t + 1, :], rim_a
-        )
-        if t == outer[min(1, tiers - 1)]:
-            send_planes(3, after)
     lift = push_c / push_b
     old = 1.0 - lift * keep_b
     now = 1.0 + keep_c + lift - push_c
     for t in range(tiers):
-        v, value = around_sum(after, t)
+        v, value = around_sum(second, t)
+        if t == 0:
+            value = value + faces[0, t] * plane_recv[3, 0]
+        if t == tiers - 1:
+            value = value + faces[1, t] * plane_recv[3, 1]
         out_ref[t] = temp[t] + old * start[t] + now * v + lift * value
         beyond_rows(
             out_ref, t, lift, row_shell[tiers + t : tiers + t + 1, :], row_shell[t : t + 1, :], rim_b
         )
-    wait_plane(3)
-    out_ref[0] = out_ref[0] + lift * faces[0, 0] * plane_recv[3, 0]
-    out_ref[tiers - 1] = out_ref[tiers - 1] + lift * faces[1, tiers - 1] * plane_recv[3, 1]
-
     bytes_of(plane_recv, halo_ssem.at[0]).wait()
     bytes_of(edge_recv, halo_ssem.at[1]).wait()
     bytes_of(rim_recv, rim_ssem).wait()
     bytes_of(gain_recv, gain_ssem).wait()
+    bytes_of(face_recv, face_ssem).wait()
     bytes_of(note_recv.at[1:], note_ssem).wait()
     bytes_of(place_recv.at[1:], place_ssem).wait()
     bytes_of(fac_recv.at[1:], fac_ssem).wait()
@@ -849,6 +897,9 @@
             pltpu.VMEM((6, 2 * tiers, cols), F32),
             pltpu.VMEM((12, 2 * tiers, cols), F32),
             pltpu.VMEM((12, 2 * tiers, cols), F32),
+            pltpu.VMEM((2, 3, rows, cols), F32),
+            pltpu.VMEM((2, 3, rows, cols), F32),
+            pltpu.VMEM((2, 3, rows, cols), F32),
             pltpu.VMEM((rows, cols), F32),
             dma((10,)),
             dma(()),
@@ -863,6 +914,8 @@
             dma(()),
             dma((2,)),
             dma((4, 2)),
+            dma(()),
+            dma(()),
             dma(()),
             dma(()),
             dma(()),

time: 28.9 us -> 27.9 us (0.965)
  Pallas kernels: 28.1 us -> 27.1 us
    pallas_call x1, Pallas kernels: 27.3 us -> 26.3 us  [shards(): pl.pallas_call(functools.partial(kernel, sizes), out_shape=(pltpu.VMEM(gr...]
where the time goes in v4:
time: 27.9 us; the launch traced here: 27.8 us
  Pallas kernels  27.1 us (97%)
  between operations  0.64 us (2%)
    pallas_call x1, Pallas kernels, shards(): pl.pallas_call(functools.partial(kernel, sizes), out_shape=(pltpu.VMEM(gr...  26.3 us
    pallas_call x1, Pallas kernels, shards(): pl.pallas_call(hand_over, out_shape=(jax.ShapeDtypeStruct(grid, F32),) *...  0.81 us

profile of v4, /device:TPU:0, one launch (start us, length us, event | category | flops | bytes accessed | tf_op | source)
XLA Modules:
  0.0 27.8 jit_solution(11517981301463615869)
XLA Ops:
  0.6 26.3 %shard_map.113 = (f32[4,128,128]{2,1,0:T(8,128)S(1)}, f32[512,128]{1,0:T(8,128)S(1)}) custom-call(f32[4,128,128]{2,1,0:T(8,128)} %temp_hbm.1, f32[4,128,128]{2,1,0:T(8,128)} %cond_hbm.1, f32[4,128,128]{2,1,0:T(8,128)} %mass_hbm.1, bf16[1,64,4096]{2,1,0:T(8,128)(2,1)} %dyn_hbm.1, bf16[1,64,4096]{2,1,0:T(8,128)(2,1)} %leak_hbm.1, s32[1,64]{1,0:T(1,128)} %bitcast.3, ...), custom_call_target="tpu_custom_call" | custom-call | tf_op jit(solution)/shard_map/pallas_call | solution.py:851
  27.0 0.8 %shard_map.114 = (f32[4,128,128]{2,1,0:T(8,128)}, f32[4,128,128]{2,1,0:T(8,128)}) custom-call(f32[4,128,128]{2,1,0:T(8,128)S(1)} %get-tuple-element.4.new, f32[4,128,128]{2,1,0:T(8,128)S(1)} %bitcast.2), custom_call_target="tpu_custom_call" | custom-call | tf_op jit(solution)/shard_map/pallas_call | solution.py:933

commit v5 on v4

--- a/solution.py
+++ b/solution.py
@@ -92,6 +92,7 @@
     diag,
     inv,
     resid,
+    column_gain,
     edge_send,
     edge_recv,
     edge_spare,
@@ -339,6 +340,20 @@
         for t in range(tiers)
     ]
 
+    sub16 = iota((4 * tiers, 2 * cols), 0)
+    lane16 = mod(iota((4 * tiers, 2 * cols), 1), cols)
+    both_picks = [
+        jnp.where(
+            ((sub16 == t) & (lane16 == 0))
+            | ((sub16 == tiers + t) & (lane16 == cols - 1))
+            | ((sub16 == 2 * tiers + t) & (lane16 == 1))
+            | ((sub16 == 3 * tiers + t) & (lane16 == cols - 2)),
+            1.0,
+            0.0,
+        ).astype(BF16)
+        for t in range(tiers)
+    ]
+
     def halo_ends(turn, field, side, lands):
         if side < 2:
             return field.at[0 if side == 0 else tiers - 1], plane_recv.at[turn, lands], 0
@@ -356,11 +371,11 @@
             for t in range(tiers):
                 edge_send[turn, 0, end * tiers + t : end * tiers + t + 1, :] = field[t, at : at + 1, :]
 
-    def columns_of(field):
-        columns = jnp.zeros((2 * tiers, rows), F32)
+    def columns_of(field, taking=picks):
+        columns = jnp.zeros((taking[0].shape[0], rows), F32)
         for t in range(tiers):
             columns = columns + lax.dot_general(
-                picks[t], two_parts(field(t), 1), (((1,), (1,)), ((), ())), preferred_element_type=F32
+                taking[t], two_parts(field(t), 1), (((1,), (1,)), ((), ())), preferred_element_type=F32
             )
         return columns
 
@@ -478,14 +493,7 @@
     fac[...] = jnp.broadcast_to(jnp.exp(sens_r * (block_sum / block_size)), (named, LANES))
 
     upper_rank = iota((8, LANES), 0) >= FOLDS
-    for tile in range(tiles):
-        fac_send[tile] = one_row(fac[tile * 8 : (tile + 1) * 8, :])
-    each_peer(lambda other: fac_copy(other).start())
-    keep(fac_send.at[me], fac_recv.at[me], fac_rsem)
-
-
-    @pl.loop(0, tiles)
-    def _(step):
+    def load_step(step):
         other = far_first(step)
 
         def factor_of(rank):
@@ -504,6 +512,12 @@
         def _():
             load_copy(other).start()
 
+    pl.loop(0, tiles // 8)(load_step)
+    for tile in range(tiles):
+        fac_send[tile] = one_row(fac[tile * 8 : (tile + 1) * 8, :])
+    each_peer(lambda other: fac_copy(other).start())
+    keep(fac_send.at[me], fac_recv.at[me], fac_rsem)
+    pl.loop(tiles // 8, tiles)(load_step)
     keep(load_send.at[me], load_recv.at[me], load_rsem)
     def missing(exists, blocks):
         @pl.when(jnp.logical_not(exists))
@@ -573,6 +587,7 @@
         scaled = push_b * inv[t]
         for k in range(6):
             faces[k, t] = scaled * faces[k, t]
+        inv[t] = inv[t] * (1.0 / middle)
 
     def layer_face(t):
         if t == 0 and t == tiers - 1:
@@ -588,6 +603,12 @@
     gain_send[3] = columns_of(lambda t: side_face[t])
     gain_send[4] = columns_of(layer_face)
     gain_send[5] = columns_of(lambda t: ends_face[t])
+    blank = jnp.zeros((rows, cols), F32)
+    column_gain[0] = columns_of(lambda t: jnp.where(col_i == 0, faces[5, t], faces[4, t]))
+    column_gain[1] = columns_of(lambda t: jnp.where(row_i == 0, 0.0, faces[2, t]))
+    column_gain[2] = columns_of(lambda t: jnp.where(row_i == rows - 1, 0.0, faces[3, t]))
+    column_gain[3] = columns_of(lambda t: faces[0, t] if t > 0 else blank)
+    column_gain[4] = columns_of(lambda t: faces[1, t] if t < tiers - 1 else blank)
     for exists, where, side in sides[:2]:
         t = 0 if side == 0 else tiers - 1
         face_send[side, 0] = faces[side, t]
@@ -653,11 +674,15 @@
     deposit(
         jnp.dot(picker, load_recv[...].reshape(sources, wide - EARLY * LANES), preferred_element_type=F32), EARLY, halves
     )
+    start, after = dirs.at[0], dirs.at[1]
+
+    def begin_rows(t, begin, end):
+        power_rows = power_ref[t * rows + begin : t * rows + end, :]
+        start[t, begin:end, :] = (resid[t, begin:end, :] + power_rows) * inv[t, begin:end, :]
+
     for t in range(tiers):
-        r = resid[t] + power_ref[t * rows : (t + 1) * rows, :]
-        resid[t] = r
-        dirs[0, t] = r * inv[t] * (1.0 / middle)
-    start, after = dirs.at[0], dirs.at[1]
+        begin_rows(t, 0, 8)
+        begin_rows(t, rows - 8, rows)
 
     def send_rims(which):
         for step, block, count, _ in which:
@@ -690,7 +715,6 @@
     own_rows = rows_of(lambda t: start[t, first, :], lambda t: start[t, last, :])
     rim_send[0] = own_rows
     send_rims(rims_of[:8])
-    send_planes(2, start)
     stay = keep_b + push_b * (middle - 1.0)
     slab_lane = iota((8, cols), 1)
 
@@ -708,15 +732,26 @@
 
     rim_send[1] = rows_of(lambda t: slab_row(t, 0, 0, 3, 7), lambda t: slab_row(t, rows - 8, 7, 2, 1))
     send_rims(rims_of[12:14])
-    own_columns = columns_of(lambda t: start[t])
+    for t in range(tiers):
+        begin_rows(t, 8, rows - 8)
+    send_planes(2, start)
+    columns = columns_of(lambda t: start[t], both_picks)
+    own_columns = columns[: 2 * tiers]
     rim_send[2] = own_columns
+    rim_send[3] = (
+        stay * own_columns
+        + column_gain[0] * columns[2 * tiers :]
+        + column_gain[1] * pltpu.roll(own_columns, 1, 1)
+        + column_gain[2] * pltpu.roll(own_columns, rows - 1, 1)
+        + column_gain[3] * pltpu.roll(own_columns, 1, 0)
+        + column_gain[4] * pltpu.roll(own_columns, 2 * tiers - 1, 0)
+    )
+    send_rims(rims_of[14:])
     send_rims(rims_of[8:12])
     for t in range(tiers):
         v, value = around_sum(start, t)
         after[t] = stay * v + value
     send_planes(3, after)
-    rim_send[3] = columns_of(lambda t: after[t])
-    send_rims(rims_of[14:])
     bytes_of(gain_recv, gain_rsem).wait()
     wait_plane(2)
     wait_plane(3)
@@ -886,6 +921,7 @@
             pltpu.VMEM(grid, F32),
             pltpu.VMEM(grid, F32),
             pltpu.VMEM(grid, F32),
+            pltpu.VMEM((5, 2 * tiers, cols), F32),
             pltpu.VMEM((2, 2, 2 * tiers, cols), F32),
             pltpu.VMEM((2, 4, 2 * tiers, cols), F32),
             pltpu.VMEM((2, 4, 2 * tiers, cols), F32),

time: 27.9 us -> 27.6 us (0.989)
  Pallas kernels: 27.1 us -> 26.8 us
    pallas_call x1, Pallas kernels: 26.3 us -> 26 us  [shards(): pl.pallas_call(functools.partial(kernel, sizes), out_shape=(pltpu.VMEM(gr...]
where the time goes in v5:
time: 27.6 us; the launch traced here: 27.5 us
  Pallas kernels  26.8 us (97%)
  between operations  0.64 us (2%)
    pallas_call x1, Pallas kernels, shards(): pl.pallas_call(functools.partial(kernel, sizes), out_shape=(pltpu.VMEM(gr...  26 us
    pallas_call x1, Pallas kernels, shards(): pl.pallas_call(hand_over, out_shape=(jax.ShapeDtypeStruct(grid, F32),) *...  0.81 us

profile of v5, /device:TPU:0, one launch (start us, length us, event | category | flops | bytes accessed | tf_op | source)
XLA Modules:
  0.0 27.5 jit_solution(6663115714724501282)
XLA Ops:
  0.6 26.0 %shard_map.113 = (f32[4,128,128]{2,1,0:T(8,128)S(1)}, f32[512,128]{1,0:T(8,128)S(1)}) custom-call(f32[4,128,128]{2,1,0:T(8,128)} %temp_hbm.1, f32[4,128,128]{2,1,0:T(8,128)} %cond_hbm.1, f32[4,128,128]{2,1,0:T(8,128)} %mass_hbm.1, bf16[1,64,4096]{2,1,0:T(8,128)(2,1)} %dyn_hbm.1, bf16[1,64,4096]{2,1,0:T(8,128)(2,1)} %leak_hbm.1, s32[1,64]{1,0:T(1,128)} %bitcast.3, ...), custom_call_target="tpu_custom_call" | custom-call | tf_op jit(solution)/shard_map/pallas_call | solution.py:886
  26.6 0.8 %shard_map.114 = (f32[4,128,128]{2,1,0:T(8,128)}, f32[4,128,128]{2,1,0:T(8,128)}) custom-call(f32[4,128,128]{2,1,0:T(8,128)S(1)} %get-tuple-element.4.new, f32[4,128,128]{2,1,0:T(8,128)S(1)} %bitcast.2), custom_call_target="tpu_custom_call" | custom-call | tf_op jit(solution)/shard_map/pallas_call | solution.py:969

commit v6 on v5

--- a/solution.py
+++ b/solution.py
@@ -173,10 +173,21 @@
         over_col = n_col - 1 - mod(turn, near) - near * div(step, tiles // 2)
         return lax.bitwise_xor(my_row, over_row) * n_col + lax.bitwise_xor(my_col, over_col)
 
-    def each_peer(act):
+    def low_first(step):
+        if n_row & (n_row - 1) or n_col & (n_col - 1) or n_row == 1 or n_col == 1:
+            return lax.rem(me + step, tiles)
+        near = n_col // 2
+        group, turn = div(step, tiles // 2), mod(step, tiles // 2)
+        over, turn = div(turn, tiles // 4), mod(turn, tiles // 4)
+        over_row = n_row // 2 - 1 - div(turn, near)
+        over_col = n_col - 1 - mod(turn, near) - near * over
+        row = group * (n_row // 2) + lax.bitwise_xor(mod(my_row, n_row // 2), over_row)
+        return row * n_col + lax.bitwise_xor(my_col, over_col)
+
+    def each_peer(act, order=far_first):
         @pl.loop(0, tiles)
         def _(step):
-            other = far_first(step)
+            other = order(step)
             pl.when(other != me)(lambda: act(other))
 
     def device(other):
@@ -328,7 +339,7 @@
 
     each_peer(lambda other: note_copy(other).start())
     keep(note_send, note_recv.at[me], note_rsem)
-    each_peer(lambda other: early_copy(other).start())
+    each_peer(lambda other: early_copy(other).start(), low_first)
     keep(early_send.at[me], early_recv.at[me], early_rsem)
 
     sub8 = iota((2 * tiers, 2 * cols), 0)
@@ -494,7 +505,7 @@
 
     upper_rank = iota((8, LANES), 0) >= FOLDS
     def load_step(step):
-        other = far_first(step)
+        other = low_first(step)
 
         def factor_of(rank):
             return fac[pl.ds(other * 8 + rank, 8, stride=0), :]
@@ -515,7 +526,7 @@
     pl.loop(0, tiles // 8)(load_step)
     for tile in range(tiles):
         fac_send[tile] = one_row(fac[tile * 8 : (tile + 1) * 8, :])
-    each_peer(lambda other: fac_copy(other).start())
+    each_peer(lambda other: fac_copy(other).start(), low_first)
     keep(fac_send.at[me], fac_recv.at[me], fac_rsem)
     pl.loop(tiles // 8, tiles)(load_step)
     keep(load_send.at[me], load_recv.at[me], load_rsem)

time: 27.6 us -> 26.8 us (0.971)
  Pallas kernels: 26.8 us -> 26 us
    pallas_call x1, Pallas kernels: 26 us -> 25.2 us  [shards(): pl.pallas_call(functools.partial(kernel, sizes), out_shape=(pltpu.VMEM(gr...]
where the time goes in v6:
time: 26.8 us; the launch traced here: 26.7 us
  Pallas kernels  26 us (97%)
  between operations  0.64 us (2%)
    pallas_call x1, Pallas kernels, shards(): pl.pallas_call(functools.partial(kernel, sizes), out_shape=(pltpu.VMEM(gr...  25.2 us
    pallas_call x1, Pallas kernels, shards(): pl.pallas_call(hand_over, out_shape=(jax.ShapeDtypeStruct(grid, F32),) *...  0.81 us

profile of v6, /device:TPU:0, one launch (start us, length us, event | category | flops | bytes accessed | tf_op | source)
XLA Modules:
  0.0 26.7 jit_solution(16668236373281653467)
XLA Ops:
  0.6 25.2 %shard_map.113 = (f32[4,128,128]{2,1,0:T(8,128)S(1)}, f32[512,128]{1,0:T(8,128)S(1)}) custom-call(f32[4,128,128]{2,1,0:T(8,128)} %temp_hbm.1, f32[4,128,128]{2,1,0:T(8,128)} %cond_hbm.1, f32[4,128,128]{2,1,0:T(8,128)} %mass_hbm.1, bf16[1,64,4096]{2,1,0:T(8,128)(2,1)} %dyn_hbm.1, bf16[1,64,4096]{2,1,0:T(8,128)(2,1)} %leak_hbm.1, s32[1,64]{1,0:T(1,128)} %bitcast.3, ...), custom_call_target="tpu_custom_call" | custom-call | tf_op jit(solution)/shard_map/pallas_call | solution.py:897
  25.9 0.8 %shard_map.114 = (f32[4,128,128]{2,1,0:T(8,128)}, f32[4,128,128]{2,1,0:T(8,128)}) custom-call(f32[4,128,128]{2,1,0:T(8,128)S(1)} %get-tuple-element.4.new, f32[4,128,128]{2,1,0:T(8,128)S(1)} %bitcast.2), custom_call_target="tpu_custom_call" | custom-call | tf_op jit(solution)/shard_map/pallas_call | solution.py:980
